TPU v7x, 512 devices: a whole 4x8x8 slice. The times are simulated.
512 devices in a mesh: gx: 32 (over x, y), gy: 16 (over z, core).
Axes of the slice: x: 4, y: 8, z: 8, core: 2. Of those that a mesh axis runs over, the one named last changes fastest.
Arguments:
- cotangent: float32 [256, 128, 512], P('gx', 'gy'), may hold values from -8 to 8
- concentration: float32 [256, 128, 512], P('gx', 'gy'), may hold values from 0.5 to 2
- conductance: float32 [256, 128, 16], P('gx', 'gy'), may hold values from 0.5 to 2
- diffusivity: float32 [32], replicated, may hold values from 30 to 10000
- rate_constant: float32 [256], replicated, may hold values from 0.02 to 0.3
- reactants: int32 [256, 2], replicated, may hold values from 0 to 31
- products: int32 [256, 2], replicated, may hold values from 0 to 31
Outputs:
- sensitivity: float32 [256, 128, 512], P('gx', 'gy')
All inputs are finite; a program needn't handle non-finite values.
Results may differ from a plain program's by a relative error of at most 0.0003.
Values sent between devices are 32-bit elements; how exact they have to be, the bound alone decides.
No kernel may reach another device: no remote copies, remote signals or barrier semaphores. Data moves between devices by JAX's collectives and lax.ppermute only.
A program may use at most 64 MiB of HBM per device.

v0:
```python
import jax
import jax.numpy as jnp
from jax import lax
from jax.sharding import PartitionSpec as P


def stoichiometry(reactants, products, species):
    species_ids = jnp.arange(species, dtype=jnp.int32)
    reactant_matrix = jnp.sum(
        (reactants[:, :, None] == species_ids[None, None, :]).astype(jnp.float32), axis=1
    )
    product_matrix = jnp.sum(
        (products[:, :, None] == species_ids[None, None, :]).astype(jnp.float32), axis=1
    )
    return (reactant_matrix, product_matrix - reactant_matrix)


def chem_adjoint(field, concentration, rate_constant, reactant_matrix, net_matrix):
    highest = lax.Precision.HIGHEST
    exponent = jnp.einsum("csz,rs->czr", jnp.log(concentration), reactant_matrix, precision=highest)
    rates = rate_constant * jnp.exp(exponent)
    inverse = 1.0 / concentration

    def transposed(vector):
        flows = jnp.einsum("csz,rs->czr", vector, net_matrix, precision=highest) * rates
        return jnp.einsum("czr,rs->csz", flows, reactant_matrix, precision=highest) * inverse

    third = field + transposed(field) / 3.0
    second = field + transposed(third) / 2.0
    return field + transposed(second)


def offset(tensor, shift_by, axis_dim):
    extent = tensor.shape[axis_dim]
    widths = [(0, 0)] * tensor.ndim
    if shift_by > 0:
        portion = lax.slice_in_dim(tensor, shift_by, extent, axis=axis_dim)
        widths[axis_dim] = (0, shift_by)
    else:
        portion = lax.slice_in_dim(tensor, 0, extent + shift_by, axis=axis_dim)
        widths[axis_dim] = (-shift_by, 0)
    return jnp.pad(portion, widths)


def local_solve(coefficient, sources, axis_dim):
    extent = coefficient.shape[axis_dim]
    diagonal = 1.0 + 2.0 * coefficient
    lower_ratio = offset(coefficient, -1, axis_dim) / diagonal
    upper_ratio = offset(coefficient, 1, axis_dim) / diagonal
    solution = sources / diagonal
    stride = 1
    while stride < extent:
        lower_before = offset(lower_ratio, -stride, axis_dim)
        upper_before = offset(upper_ratio, -stride, axis_dim)
        lower_after = offset(lower_ratio, stride, axis_dim)
        upper_after = offset(upper_ratio, stride, axis_dim)
        denominator = 1.0 - lower_ratio * upper_before - upper_ratio * lower_after
        solution = (
            solution
            + lower_ratio * offset(solution, -stride, axis_dim + 1)
            + upper_ratio * offset(solution, stride, axis_dim + 1)
        ) / denominator
        lower_ratio, upper_ratio = (
            lower_ratio * lower_before / denominator,
            upper_ratio * upper_after / denominator,
        )
        stride = stride * 2
    return solution


def mat_product(left_mat, right_mat):
    return (
        left_mat[0] * right_mat[0] + left_mat[1] * right_mat[2],
        left_mat[0] * right_mat[1] + left_mat[1] * right_mat[3],
        left_mat[2] * right_mat[0] + left_mat[3] * right_mat[2],
        left_mat[2] * right_mat[1] + left_mat[3] * right_mat[3],
    )


def mat_vector(left_mat, vector):
    return (
        left_mat[0] * vector[0] + left_mat[1] * vector[1],
        left_mat[2] * vector[0] + left_mat[3] * vector[1],
    )


def build_stack(rows_six):
    zeroes = jnp.zeros_like(rows_six[0])
    return jnp.stack(
        [
            zeroes,
            rows_six[2],
            zeroes,
            rows_six[3],
            rows_six[4],
            zeroes,
            rows_six[5],
            zeroes,
            rows_six[0],
            rows_six[1],
        ]
    )


def block_reduce(coeffs, neighbour, count):
    stride = 1
    while stride < count:
        before = neighbour(coeffs, -stride)
        after = neighbour(coeffs, stride)
        own_left = (coeffs[0], coeffs[1], coeffs[2], coeffs[3])
        own_right = (coeffs[4], coeffs[5], coeffs[6], coeffs[7])
        left_before = (before[0], before[1], before[2], before[3])
        right_before = (before[4], before[5], before[6], before[7])
        left_after = (after[0], after[1], after[2], after[3])
        right_after = (after[4], after[5], after[6], after[7])
        first_term = mat_product(own_left, right_before)
        second_term = mat_product(own_right, left_after)
        system = (
            1.0 - first_term[0] - second_term[0],
            -first_term[1] - second_term[1],
            -first_term[2] - second_term[2],
            1.0 - first_term[3] - second_term[3],
        )
        determinant = system[0] * system[3] - system[1] * system[2]
        inverse = (
            system[3] / determinant,
            -system[1] / determinant,
            -system[2] / determinant,
            system[0] / determinant,
        )
        pushed_before = mat_vector(own_left, (before[8], before[9]))
        pushed_after = mat_vector(own_right, (after[8], after[9]))
        sources = (
            coeffs[8] + pushed_before[0] + pushed_after[0],
            coeffs[9] + pushed_before[1] + pushed_after[1],
        )
        new_left = mat_product(inverse, mat_product(own_left, left_before))
        new_right = mat_product(inverse, mat_product(own_right, right_after))
        new_values = mat_vector(inverse, sources)
        coeffs = jnp.stack(list(new_left) + list(new_right) + list(new_values))
        stride = stride * 2
    return (coeffs[8], coeffs[9])


def solve_gathered(received):

    def local_neighbour(coeffs, shift_by):
        return offset(coeffs, shift_by, 1)

    first_value, last_value = block_reduce(
        build_stack(received), local_neighbour, received.shape[1]
    )
    return jnp.stack([offset(last_value, -1, 0), offset(first_value, 1, 0)])


def line_pass(field, coefficient, axis_dim, reduce_fn):
    shape = field.shape
    extent = shape[axis_dim]
    position = lax.broadcasted_iota(jnp.int32, shape, axis_dim)
    sources = jnp.stack(
        [field, (position == 0).astype(jnp.float32), (position == extent - 1).astype(jnp.float32)]
    )
    solved = local_solve(coefficient, sources, axis_dim)

    def edge(tensor, index):
        return lax.index_in_dim(tensor, index, axis_dim, keepdims=False).reshape(-1)

    first_coef = edge(coefficient, 0)
    last_coef = edge(coefficient, extent - 1)
    rows_six = (
        first_coef * edge(solved[0], 0),
        last_coef * edge(solved[0], extent - 1),
        first_coef * edge(solved[1], 0),
        last_coef * edge(solved[1], extent - 1),
        first_coef * edge(solved[2], 0),
        last_coef * edge(solved[2], extent - 1),
    )
    from_left, from_right = reduce_fn(rows_six)
    edge_shape = list(shape)
    edge_shape[axis_dim] = 1
    return (
        solved[0]
        + from_left.reshape(edge_shape) * solved[1]
        + from_right.reshape(edge_shape) * solved[2]
    )


def on_device(
    cotangent, concentration, conductance, diffusivity, rate_constant, reactants, products
):
    rows_x, rows_y, width = cotangent.shape
    depth = conductance.shape[2]
    species = diffusivity.shape[0]
    coefficient = (conductance[:, :, None, :] * diffusivity[None, None, :, None]).reshape(
        rows_x, rows_y, width
    )
    reactant_matrix, net_matrix = stoichiometry(reactants, products, species)

    def reduce_y(rows_six):
        members = lax.axis_size("gy")
        outgoing = jnp.stack(rows_six).reshape(6, 1, members, -1)
        solved = solve_gathered(
            lax.all_to_all(outgoing, "gy", split_axis=2, concat_axis=1, tiled=True)
        )
        returned = lax.all_to_all(solved, "gy", split_axis=1, concat_axis=2, tiled=True).reshape(
            2, -1
        )
        return (returned[0], returned[1])

    def reduce_x(rows_six):
        members = lax.axis_size("gx")
        outgoing = jnp.stack(rows_six).reshape(6, 1, members, -1)
        solved = solve_gathered(
            lax.all_to_all(outgoing, "gx", split_axis=2, concat_axis=1, tiled=True)
        )
        returned = lax.all_to_all(solved, "gx", split_axis=1, concat_axis=2, tiled=True).reshape(
            2, -1
        )
        return (returned[0], returned[1])

    after_y = line_pass(cotangent, coefficient, 1, reduce_y)
    cells = after_y.reshape(rows_x * rows_y, species, depth)
    conc_cells = concentration.reshape(rows_x * rows_y, species, depth)
    after_chem = chem_adjoint(
        cells, conc_cells, rate_constant, reactant_matrix, net_matrix
    ).reshape(rows_x, rows_y, width)
    return line_pass(after_chem, coefficient, 0, reduce_x)


def solution(mesh):
    placed = (P("gx", "gy", None), P("gx", "gy", None), P("gx", "gy", None), P(), P(), P(), P())
    return jax.shard_map(
        on_device, mesh=mesh, in_specs=placed, out_specs=P("gx", "gy", None), check_vma=False
    )
```

profile of v0, /device:TPU:64, one launch (start us, length us, event | category | flops | bytes accessed | tf_op | source)
XLA Modules:
  0.0 107.1 jit_solution(7198714826743079957)
XLA Ops:
  0.7 0.9 broadcast_multiply_fusion
  4.3 0.8 copy-done.19
  7.1 0.8 fusion.417
  11.6 10.0 %all-to-all-start = ((f32[6,1,16,256]{3,1,0,2:T(1,128)}), f32[6,1,16,256]{3,1,0,2:T(1,128)S(1)}, u32[]{:S(2)}, u32[]{:S(2)}) async-start(f32[6,1,16,256]{3,1,0,2:T(1,128)} %constant_dynamic-update-slice_fusion), calls=%async_computation | async-start | bytes 196608 | tf_op jit(solution)/shard_map/all_to_all | solution.py:203
  21.6 0.7 fusion.434
  26.2 1.1 fusion.1
  27.3 0.7 fusion.411
  34.9 6.8 %all-to-all-start.1 = ((f32[2,16,1,256]{3,2,0,1:T(1,128)}), f32[2,16,1,256]{3,2,0,1:T(1,128)S(1)}, u32[]{:S(2)}, u32[]{:S(2)}) async-start(f32[2,16,1,256]{3,2,0,1:T(1,128)} %copy.155), calls=%async_computation.1 | async-start | bytes 65536 | tf_op jit(solution)/shard_map/all_to_all | solution.py:205
  41.8 0.7 multiply_subtract_fusion
  43.1 1.4 %copy.160 = f32[64,32,16]{0,1,2:T(8,128)} copy(f32[64,32,16]{2,1,0:T(8,128)S(1)} %squeeze.555) | data formatting | bytes 262144 | tf_op jit(solution)/shard_map/squeeze | solution.py:175
  44.9 1.4 %copy.158 = f32[64,32,16]{0,1,2:T(8,128)} copy(f32[64,32,16]{2,1,0:T(8,128)S(1)} %squeeze.488) | data formatting | bytes 262144 | tf_op jit(solution)/shard_map/squeeze | solution.py:182
  46.6 1.4 %copy.157 = f32[64,32,16]{0,1,2:T(8,128)} copy(f32[64,32,16]{2,1,0:T(8,128)S(1)} %squeeze.554) | data formatting | bytes 262144 | tf_op jit(solution)/shard_map/squeeze | solution.py:173
  48.0 1.3 %div.1724 = f32[64,32,16]{2,1,0:T(8,128)S(1)} reshape(f32[8,8,512]{2,1,0:T(8,128)} %get-tuple-element.472) | data formatting | bytes 262144 | tf_op jit(solution)/shard_map/div | solution.py:22
  51.5 1.4 %copy.159 = f32[64,32,16]{0,1,2:T(8,128)} copy(f32[64,32,16]{2,1,0:T(8,128)S(1)} %mul.19200) | data formatting | bytes 262144 | tf_op jit(solution)/shard_map/mul | solution.py:184
  53.3 1.4 %copy.156 = f32[64,32,16]{0,1,2:T(8,128)} copy(f32[64,32,16]{2,1,0:T(8,128)S(1)} %mul.19196) | data formatting | bytes 262144 | tf_op jit(solution)/shard_map/mul | solution.py:183
  54.6 1.2 %multiply_add_fusion = f32[64,32,16]{0,1,2:T(8,128)S(1)} fusion(f32[64,32,16]{0,1,2:T(8,128)} %copy.159, f32[64,32,16]{0,1,2:T(8,128)S(1)} %copy-done.15, f32[64,32,16]{0,1,2:T(8,128)S(1)} %copy-done.16, f32[64,32,16]{0,1,2:T(8,128)} %copy.156, f32[64,32,16]{0,1,2:T(8,128)S(1)} %copy-done.17), kind=kLoop, calls=%fused_computation.48 | loop fusion | flops 131072 | bytes 786432 | tf_op jit(solution)/shard_map/add | solution.py:182
  55.8 1.1 convolution_multiply_fusion.2
  56.9 1.5 %fusion.4 = f32[64,32,16]{0,1,2:T(8,128)S(1)} fusion(f32[64,32,16]{0,1,2:T(8,128)S(1)} %multiply_add_fusion, f32[64,32,16]{0,1,2:T(8,128)S(1)} %copy.162, f32[64,16,256]{2,0,1:T(8,128)S(1)} %convolution_multiply_fusion.2, f32[256,32]{0,1:T(8,128)S(1)} %get-tuple-element.510), kind=kOutput, calls=%fused_computation.11 | convolution fusion | flops 100761600 | bytes 1474560 | tf_op jit(solution)/shard_map/czr,rs->csz/dot_general | solution.py:26
  58.4 1.1 convolution_multiply_fusion.1
  59.5 1.5 %fusion.7 = f32[64,32,16]{0,1,2:T(8,128)S(1)} fusion(f32[64,32,16]{0,1,2:T(8,128)S(1)} %multiply_add_fusion, f32[64,32,16]{0,1,2:T(8,128)S(1)} %copy.162, f32[64,16,256]{2,0,1:T(8,128)S(1)} %convolution_multiply_fusion.1, f32[256,32]{0,1:T(8,128)S(1)} %get-tuple-element.510), kind=kOutput, calls=%fused_computation.14 | convolution fusion | flops 100761600 | bytes 1474560 | tf_op jit(solution)/shard_map/czr,rs->csz/dot_general | solution.py:26
  61.1 1.1 convolution_multiply_fusion
  62.1 1.8 %fusion.9 = f32[64,32,16]{0,1,2:T(8,128)S(1)} fusion(f32[64,32,16]{0,1,2:T(8,128)S(1)} %multiply_add_fusion, f32[64,32,16]{0,1,2:T(8,128)S(1)} %copy.162, f32[64,16,256]{2,0,1:T(8,128)S(1)} %convolution_multiply_fusion, f32[256,32]{0,1:T(8,128)S(1)} %get-tuple-element.510), kind=kOutput, calls=%fused_computation.16 | convolution fusion | flops 100728832 | bytes 1474560 | tf_op jit(solution)/shard_map/czr,rs->csz/dot_general | solution.py:26
  63.9 0.9 copy.165
  65.7 0.8 copy-done.1
  66.6 0.8 copy-done.3
  67.7 0.8 copy-done.5
  68.8 0.8 copy-done.7
  70.1 0.7 copy.166
  70.8 9.9 %all-to-all-start.2 = ((f32[6,1,32,128]{3,1,0,2:T(1,128)}), f32[6,1,32,128]{3,1,0,2:T(1,128)S(1)}, u32[]{:S(2)}, u32[]{:S(2)}) async-start(f32[6,1,32,128]{3,1,0,2:T(1,128)} %copy.166), calls=%async_computation.2 | async-start | bytes 196608 | tf_op jit(solution)/shard_map/all_to_all | solution.py:214
  80.8 10.1 %all-to-all-done.2 = f32[6,1,32,128]{3,1,0,2:T(1,128)S(1)} async-done(((f32[6,1,32,128]{3,1,0,2:T(1,128)}), f32[6,1,32,128]{3,1,0,2:T(1,128)S(1)}, u32[]{:S(2)}, u32[]{:S(2)}) %all-to-all-start.2) | async-done | bytes 98336 | tf_op jit(solution)/shard_map/all_to_all | solution.py:214
  93.0 13.3 %all_to_all.16 = f32[2,32,1,128]{3,2,0,1:T(1,128)S(1)} all-to-all(f32[2,32,1,128]{3,2,0,1:T(1,128)S(1)} %copy.172), channel_id=1, replica_groups=mesh['gx'=32,'gy'=16] {'gx'}, dimensions={1} | all-to-all | bytes 65536 | tf_op jit(solution)/shard_map/all_to_all | solution.py:216
  106.4 0.7 fusion.11
  (299 shorter events, 26.7 us)
Async XLA Ops:
  2.3 0.8 copy-start.27
  4.0 1.7 %copy-start.2 = (f32[8,8,512]{2,1,0:T(8,128)}, f32[8,8,512]{2,1,0:T(8,128)S(1)}, u32[]{:S(2)}) copy-start(f32[8,8,512]{2,1,0:T(8,128)S(1)} %get-tuple-element.232) | copy-start | bytes 393220
  4.1 1.2 %copy-start = (f32[8,8,512]{2,1,0:T(8,128)}, f32[8,8,512]{2,1,0:T(8,128)S(1)}, u32[]{:S(2)}) copy-start(f32[8,8,512]{2,1,0:T(8,128)S(1)} %get-tuple-element.470) | copy-start | bytes 393220
  4.1 1.0 copy-start.19
  5.8 17.6 %copy-start.4 = (f32[8,8,512]{2,1,0:T(8,128)}, f32[8,8,512]{2,1,0:T(8,128)S(1)}, u32[]{:S(2)}) copy-start(f32[8,8,512]{2,1,0:T(8,128)S(1)} %get-tuple-element.230) | copy-start | bytes 393220
  11.0 10.6 %copy-start.26 = (f32[8,8,512]{2,1,0:T(8,128)S(1)}, f32[8,8,512]{2,1,0:T(8,128)}, u32[]{:S(2)}) copy-start(f32[8,8,512]{2,1,0:T(8,128)} %param.8) | copy-start | bytes 393220
  11.6 16.7 %all-to-all-start = ((f32[6,1,16,256]{3,1,0,2:T(1,128)}), f32[6,1,16,256]{3,1,0,2:T(1,128)S(1)}, u32[]{:S(2)}, u32[]{:S(2)}) async-start(f32[6,1,16,256]{3,1,0,2:T(1,128)} %constant_dynamic-update-slice_fusion), calls=%async_computation | async-start | bytes 196608 | tf_op jit(solution)/shard_map/all_to_all | solution.py:203
  23.5 18.3 %copy-start.6 = (f32[8,8,512]{2,1,0:T(8,128)}, f32[8,8,512]{2,1,0:T(8,128)S(1)}, u32[]{:S(2)}) copy-start(f32[8,8,512]{2,1,0:T(8,128)S(1)} %get-tuple-element.228) | copy-start | bytes 393220
  24.1 0.7 copy-start.29
  24.1 0.7 copy-start.30
  25.5 0.7 copy-start.31
  34.2 7.6 %copy-start.9 = (f32[8,8,512]{2,1,0:T(8,128)S(1)}, f32[8,8,512]{2,1,0:T(8,128)}, u32[]{:S(2)}) copy-start(f32[8,8,512]{2,1,0:T(8,128)} %copy-done.8) | copy-start | bytes 393220
  34.3 7.5 %slice-start = ((f32[8,8,512]{2,1,0:T(8,128)}), f32[4,8,512]{2,1,0:T(8,128)S(1)}, s32[]{:S(2)}) async-start(f32[8,8,512]{2,1,0:T(8,128)} %copy-done.8), calls=%async_computation.4 | async-start | bytes 131072 | tf_op jit(solution)/shard_map/slice | solution.py:40
  34.9 16.1 %all-to-all-start.1 = ((f32[2,16,1,256]{3,2,0,1:T(1,128)}), f32[2,16,1,256]{3,2,0,1:T(1,128)S(1)}, u32[]{:S(2)}, u32[]{:S(2)}) async-start(f32[2,16,1,256]{3,2,0,1:T(1,128)} %copy.155), calls=%async_computation.1 | async-start | bytes 65536 | tf_op jit(solution)/shard_map/all_to_all | solution.py:205
  41.8 0.9 copy-start.22
  43.1 1.4 %copy-start.21 = (f32[1,8,8,512]{3,2,1,0:T(8,128)S(1)}, f32[1,8,8,512]{3,2,1,0:T(8,128)}, u32[]{:S(2)}) copy-start(f32[1,8,8,512]{3,2,1,0:T(8,128)} %get-tuple-element.407) | copy-start | bytes 393220
  44.8 1.4 %copy-start.20 = (f32[1,8,8,512]{3,2,1,0:T(8,128)S(1)}, f32[1,8,8,512]{3,2,1,0:T(8,128)}, u32[]{:S(2)}) copy-start(f32[1,8,8,512]{3,2,1,0:T(8,128)} %get-tuple-element.402) | copy-start | bytes 393220
  49.3 0.9 copy-start.25
  49.9 0.9 copy-start.24
  53.2 1.4 %copy-start.15 = (f32[64,32,16]{0,1,2:T(8,128)S(1)}, f32[64,32,16]{0,1,2:T(8,128)}, u32[]{:S(2)}) copy-start(f32[64,32,16]{0,1,2:T(8,128)} %copy.160) | copy-start | bytes 393220
  53.2 1.4 %copy-start.16 = (f32[64,32,16]{0,1,2:T(8,128)S(1)}, f32[64,32,16]{0,1,2:T(8,128)}, u32[]{:S(2)}) copy-start(f32[64,32,16]{0,1,2:T(8,128)} %copy.158) | copy-start | bytes 393220
  53.2 1.4 %copy-start.17 = (f32[64,32,16]{0,1,2:T(8,128)S(1)}, f32[64,32,16]{0,1,2:T(8,128)}, u32[]{:S(2)}) copy-start(f32[64,32,16]{0,1,2:T(8,128)} %copy.157) | copy-start | bytes 393220
  54.6 1.2 %copy-start.18 = (f32[256,32]{0,1:T(8,128)S(1)}, f32[256,32]{0,1:T(8,128)}, u32[]{:S(2)}) copy-start(f32[256,32]{0,1:T(8,128)} %get-tuple-element.509) | copy-start | bytes 98308
  65.5 0.9 copy-start.1
  66.5 0.9 copy-start.3
  66.5 1.0 copy-start.14
  67.6 0.9 copy-start.5
  67.6 1.0 copy-start.12
  68.7 0.9 copy-start.7
  68.7 1.0 copy-start.10
  68.8 1.0 copy-start.23
  70.8 20.1 %all-to-all-start.2 = ((f32[6,1,32,128]{3,1,0,2:T(1,128)}), f32[6,1,32,128]{3,1,0,2:T(1,128)S(1)}, u32[]{:S(2)}, u32[]{:S(2)}) async-start(f32[6,1,32,128]{3,1,0,2:T(1,128)} %copy.166), calls=%async_computation.2 | async-start | bytes 196608 | tf_op jit(solution)/shard_map/all_to_all | solution.py:214
  (4 other events, 2.6 us)
where the time goes:
time: 108 us; the launch traced here: 107 us
  local copies, waits for them, and re-layouts  33 us (31%)
  starting transfers between devices  26.8 us (25%)
  blocking collectives  13.3 us (12%)
  other arithmetic  12.8 us (12%)
  waiting for transfers between devices  10.5 us (10%)
  matrix products  9.12 us (8%)
  between operations  1.62 us (2%)
    all_to_all x1, blocking collectives, reduce_x(): lax.all_to_all(solved, 'gx', split_axis=1, concat_axis=2, tiled=True)  13.3 us
    unnamed x88, local copies, waits for them, and re-layouts  12.1 us
    all_to_all x1, waiting for transfers between devices, reduce_x(): lax.all_to_all(outgoing, 'gx', split_axis=2, concat_axis=1, tiled=True)  10.1 us
    all_to_all x1, starting transfers between devices, reduce_y(): lax.all_to_all(outgoing, 'gy', split_axis=2, concat_axis=1, tiled=True)  9.98 us
    all_to_all x1, starting transfers between devices, reduce_x(): lax.all_to_all(outgoing, 'gx', split_axis=2, concat_axis=1, tiled=True)  9.95 us
    all_to_all x1, starting transfers between devices, reduce_y(): lax.all_to_all(solved, 'gy', split_axis=1, concat_axis=2, tiled=True)  6.85 us
    dot_general x3, matrix products, transposed(): jnp.einsum('czr,rs->csz', flows, reactant_matrix, precision=highest)  4.89 us
    dot_general x3, matrix products, transposed(): jnp.einsum('csz,rs->czr', vector, net_matrix, precision=highest) * rates  3.17 us
  transfers between devices with their start and end apart: 3, of which 2 were waited for; matrix products, arithmetic and copies ran while one was open for 11% of the time, Pallas kernels for 0%

commit v1 on v0

v1 whole, which is shorter than its diff:
```python
import functools

import jax
import jax.numpy as jnp
from jax import lax
from jax.experimental import pallas as pl
from jax.experimental.pallas import tpu as pltpu
from jax.sharding import PartitionSpec as P


CELLS = 8
LANES = 128


def call(kernel, out_shape, scratch_shapes=()):
    whole = pl.BlockSpec(memory_space=pltpu.VMEM)

    def run(*operands):
        outs = jax.tree.map(lambda _: whole, out_shape)
        return pl.pallas_call(
            kernel,
            out_shape=out_shape,
            in_specs=[whole] * len(operands),
            out_specs=outs,
            scratch_shapes=list(scratch_shapes),
        )(*operands)

    return run


def struct(*shape):
    return jax.ShapeDtypeStruct(shape, jnp.float32)


def spread(packed, cell, depth):
    lane = lax.broadcasted_iota(jnp.int32, packed.shape, 1)
    index = lax.rem(lane, depth) + cell * depth
    return jnp.take_along_axis(packed, index, axis=1, mode="promise_in_bounds")


def wide(tile, width):
    return jnp.concatenate([tile] * (width // LANES), axis=1)


def expand_all(gathered_ref, tiles_ref, blocks, depth):
    def body(block, carry):
        packed = 1.0 / gathered_ref[block]
        for cell in range(CELLS):
            tiles_ref[block * CELLS + cell] = spread(packed, cell, depth)
        return carry

    lax.fori_loop(0, blocks, body, 0)


def shoot(tiles_ref, inverse_rate, left_ref, left_step_ref, right_ref, right_step_ref, blocks):
    width = inverse_rate.shape[1]
    ones = jnp.ones_like(inverse_rate)

    def body(block, carry):
        left, left_step, right, right_step = carry
        mirror = blocks - 1 - block
        left_ref[block] = left
        left_step_ref[block] = left_step
        right_ref[mirror] = right
        right_step_ref[mirror] = right_step
        for cell in range(CELLS):
            ahead = wide(tiles_ref[block * CELLS + cell], width) * inverse_rate
            behind = wide(tiles_ref[mirror * CELLS + CELLS - 1 - cell], width) * inverse_rate
            left_step = left_step + ahead * left
            left = left + left_step
            right_step = right_step + behind * right
            right = right + right_step
        return left, left_step, right, right_step

    left, _, right, _ = lax.fori_loop(0, blocks, body, (ones, ones, ones, ones))
    left_ref[blocks] = left
    right_ref[blocks] = right


def own_block(tiles_ref, inverse_rate, left_ref, left_step_ref, right_ref, right_step_ref, me):
    width = inverse_rate.shape[1]
    rates = [wide(tiles_ref[me * CELLS + cell], width) * inverse_rate for cell in range(CELLS)]

    def sweep(value, step, order):
        ratios, gaps = [None] * CELLS, [None] * CELLS
        reciprocal = 1.0 / value
        for cell in order:
            gaps[cell] = step * reciprocal
            step = step + rates[cell] * value
            following = value + step
            reciprocal = 1.0 / following
            ratios[cell] = value * reciprocal
            value = following
        return ratios, gaps

    forward, left_gaps = sweep(left_ref[me], left_step_ref[me], range(CELLS))
    backward, right_gaps = sweep(right_ref[me], right_step_ref[me], reversed(range(CELLS)))
    gains = [
        rates[cell] / (rates[cell] + left_gaps[cell] + right_gaps[cell]) for cell in range(CELLS)
    ]
    return forward, backward, gains


def sweeps(sources, forward, backward, from_left, from_right):
    before, after = [None] * CELLS, [None] * CELLS
    running = from_left
    for cell in range(CELLS):
        before[cell] = running
        running = forward[cell] * (sources[cell] + running)
    last = running
    running = from_right
    for cell in reversed(range(CELLS)):
        after[cell] = running
        running = backward[cell] * (sources[cell] + running)
    return before, after, last, running


def start_kernel(depth, members, cot_ref, cond_ref, inverse_ref, send_ref, lines_ref):
    width = cot_ref.shape[2]
    inverse_rate = jnp.broadcast_to(inverse_ref[...], (CELLS, width))
    packed = 1.0 / cond_ref[...]
    lines = jnp.swapaxes(cot_ref[...], 0, 1)
    lines_ref[...] = lines
    sources = [lines[cell] for cell in range(CELLS)]
    rates = [wide(spread(packed, cell, depth), width) * inverse_rate for cell in range(CELLS)]

    def project(order):
        value = jnp.ones_like(inverse_rate)
        step = value
        total = jnp.zeros_like(value)
        for cell in order:
            total = total + value * sources[cell]
            step = step + rates[cell] * value
            value = value + step
        return total / value

    last = project(range(CELLS))
    first = project(reversed(range(CELLS)))
    for member in range(members):
        send_ref[member, :, :width] = first
        send_ref[member, :, width : 2 * width] = last
        send_ref[member, :, 2 * width :] = cond_ref[...]


def to_species(cells, turn_ref, depth):
    rows = cells.shape[0]
    turn_ref[...] = jnp.concatenate([cells, cells], axis=0).T
    species = cells.shape[1] // depth
    low = lax.broadcasted_iota(jnp.int32, (species, 2 * rows), 1) < rows
    pairs = []
    for pair in range(depth // 2):
        even = turn_ref[pl.ds(2 * pair, species, stride=depth), :]
        odd = turn_ref[pl.ds(2 * pair + 1, species, stride=depth), :]
        pairs.append(jnp.where(low, even, odd))
    return pairs


def from_species(pairs, turn_ref, depth):
    species, columns = pairs[0].shape
    for pair, tile in enumerate(pairs):
        turn_ref[pl.ds(2 * pair, species, stride=depth), :] = tile
        turn_ref[pl.ds(2 * pair + 1, species, stride=depth), :] = pltpu.roll(
            tile, columns // 2, 1
        )
    return turn_ref[...].T[: columns // 2]


def halves(value):
    high = value.astype(jnp.bfloat16)
    return high, (value - high.astype(jnp.float32)).astype(jnp.bfloat16)


def counts(pair_ref, species):
    ids = lax.broadcasted_iota(jnp.int32, (pair_ref.shape[0], species), 1)
    return (pair_ref[:, 0:1] == ids).astype(jnp.float32) + (pair_ref[:, 1:2] == ids).astype(
        jnp.float32
    )


def rates_kernel(
    depth, conc_ref, rate_ref, reactants_ref, products_ref, rates_ref, inverse_ref, net_ref,
    back_ref, turn_ref,
):
    rows_x, rows_y, width = conc_ref.shape
    species = width // depth
    used = counts(reactants_ref, species)
    net = (counts(products_ref, species) - used).astype(jnp.bfloat16)
    net_ref[...] = jnp.concatenate([net, net], axis=1)
    back_ref[...] = used.T.astype(jnp.bfloat16)
    used = used.astype(jnp.bfloat16)
    used = jnp.concatenate([used, used], axis=1)
    constant = rate_ref[...]
    pairs = to_species(conc_ref[...].reshape(rows_x * rows_y, width), turn_ref, depth)
    for pair, conc in enumerate(pairs):
        columns = pl.ds(pair * conc.shape[1], conc.shape[1])
        inverse_ref[:, columns] = 1.0 / conc
        stacked = jnp.concatenate(halves(jnp.log(conc)), axis=0)
        exponent = jnp.dot(used, stacked, preferred_element_type=jnp.float32)
        rates_ref[:, columns] = constant * jnp.exp(exponent)


def chemistry(field, rates, inverse, net, back):
    def transposed(vector):
        stacked = jnp.concatenate(halves(vector), axis=0)
        flows = jnp.dot(net, stacked, preferred_element_type=jnp.float32) * rates
        high, low = halves(flows)
        gathered = jnp.dot(back, high, preferred_element_type=jnp.float32) + jnp.dot(
            back, low, preferred_element_type=jnp.float32
        )
        return gathered * inverse

    third = field + transposed(field) * (1.0 / 3.0)
    second = field + transposed(third) * 0.5
    return field + transposed(second)


def weights_kernel(
    depth, blocks, axis, gathered_ref, inverse_ref, weight_ref, forward_ref, backward_ref,
    gain_ref, tiles_ref, left_ref, left_step_ref, right_ref, right_step_ref,
):
    me = lax.axis_index(axis)
    width = inverse_ref.shape[1]
    inverse_rate = jnp.broadcast_to(inverse_ref[...], (CELLS, width))
    expand_all(gathered_ref, tiles_ref, blocks, depth)
    shoot(tiles_ref, inverse_rate, left_ref, left_step_ref, right_ref, right_step_ref, blocks)
    left_scale = 1.0 / left_ref[me]
    right_scale = 1.0 / right_ref[me]

    def lower(block, carry):
        weight_ref[block] = left_ref[block + 1] * left_scale
        return carry

    def upper(block, carry):
        weight_ref[block] = right_ref[block - 1] * right_scale
        return carry

    lax.fori_loop(0, me, lower, 0)
    lax.fori_loop(me + 1, blocks, upper, 0)
    weight_ref[me] = jnp.zeros_like(left_scale)
    forward, backward, gains = own_block(
        tiles_ref, inverse_rate, left_ref, left_step_ref, right_ref, right_step_ref, me
    )
    for cell in range(CELLS):
        forward_ref[cell] = forward[cell]
        backward_ref[cell] = backward[cell]
        gain_ref[cell] = gains[cell]


def middle_kernel(
    depth, blocks, axis, next_blocks, next_axis, received_ref, lines_ref, inverse_ref, rates_ref,
    inverse_conc_ref, net_ref, back_ref, forward_ref, backward_ref, send_ref, sources_ref,
    cond_ref, tiles_ref, left_ref, left_step_ref, right_ref, right_step_ref, turn_ref,
):
    me = lax.axis_index(axis)
    width = inverse_ref.shape[1]
    inverse_rate = jnp.broadcast_to(inverse_ref[...], (CELLS, width))
    cond_ref[...] = received_ref[:, :, 2 * width :]
    expand_all(cond_ref, tiles_ref, blocks, depth)
    shoot(tiles_ref, inverse_rate, left_ref, left_step_ref, right_ref, right_step_ref, blocks)

    def lower(block, total):
        first = received_ref[block, :, :width]
        last = received_ref[block, :, width : 2 * width]
        outside = left_ref[block] - left_step_ref[block]
        return total + outside * first + left_ref[block + 1] * last

    def upper(block, total):
        first = received_ref[block, :, :width]
        last = received_ref[block, :, width : 2 * width]
        outside = right_ref[block] - right_step_ref[block]
        return total + right_ref[block - 1] * first + outside * last

    zero = jnp.zeros_like(inverse_rate)
    from_left = lax.fori_loop(0, me, lower, zero) / left_ref[me]
    from_right = lax.fori_loop(me + 1, blocks, upper, zero) / right_ref[me]
    forward, backward, gains = own_block(
        tiles_ref, inverse_rate, left_ref, left_step_ref, right_ref, right_step_ref, me
    )
    sources = [lines_ref[cell] for cell in range(CELLS)]
    before, after, _, _ = sweeps(sources, forward, backward, from_left, from_right)
    solved = jnp.stack(
        [(sources[k] + before[k] + after[k]) * gains[k] for k in range(CELLS)], axis=0
    )
    solved = jnp.swapaxes(solved, 0, 1).reshape(CELLS * CELLS, width)

    net = net_ref[...]
    back = back_ref[...]
    pairs = to_species(solved, turn_ref, depth)
    columns = pairs[0].shape[1]
    done = []
    for chunk in range(len(pairs) // 2):
        at = pl.ds(chunk * 2 * columns, 2 * columns)
        field = jnp.concatenate(pairs[2 * chunk : 2 * chunk + 2], axis=1)
        result = chemistry(field, rates_ref[:, at], inverse_conc_ref[:, at], net, back)
        done += [result[:, :columns], result[:, columns:]]
    changed = from_species(done, turn_ref, depth).reshape(CELLS, CELLS, width)
    sources_ref[...] = changed
    _, _, last, first = sweeps(
        [changed[k] for k in range(CELLS)],
        [forward_ref[k] for k in range(CELLS)],
        [backward_ref[k] for k in range(CELLS)],
        zero,
        zero,
    )
    here = lax.axis_index(next_axis)

    def to_earlier(block, carry):
        send_ref[block] = first
        return carry

    def to_later(block, carry):
        send_ref[block] = last
        return carry

    lax.fori_loop(0, here + 1, to_earlier, 0)
    lax.fori_loop(here + 1, next_blocks, to_later, 0)


def finish_kernel(
    blocks, axis, received_ref, weight_ref, sources_ref, forward_ref, backward_ref, gain_ref,
    out_ref,
):
    me = lax.axis_index(axis)
    zero = jnp.zeros_like(weight_ref[0])

    def add(block, total):
        return total + weight_ref[block] * received_ref[block]

    from_left = lax.fori_loop(0, me, add, zero)
    from_right = lax.fori_loop(me + 1, blocks, add, zero)
    sources = [sources_ref[k] for k in range(CELLS)]
    before, after, _, _ = sweeps(
        sources,
        [forward_ref[k] for k in range(CELLS)],
        [backward_ref[k] for k in range(CELLS)],
        from_left,
        from_right,
    )
    for k in range(CELLS):
        out_ref[k] = (sources[k] + before[k] + after[k]) * gain_ref[k]


def on_device(
    cotangent, concentration, conductance, diffusivity, rate_constant, reactants, products
):
    rows_x, rows_y, width = cotangent.shape
    depth = conductance.shape[2]
    species = diffusivity.shape[0]
    reactions = rate_constant.shape[0]
    across_x = lax.axis_size("gx")
    across_y = lax.axis_size("gy")
    packed_y = conductance.reshape(rows_x, rows_y * depth)
    packed_x = jnp.swapaxes(conductance, 0, 1).reshape(rows_y, rows_x * depth)
    inverse_rate = jnp.repeat(1.0 / diffusivity, depth)[None, :]

    def shots(blocks):
        edge = pltpu.VMEM((blocks + 1, CELLS, width), jnp.float32)
        return [pltpu.VMEM((blocks * CELLS, CELLS, LANES), jnp.float32)] + [edge] * 4

    turn = pltpu.VMEM((width, 2 * rows_x * rows_y), jnp.float32)
    block = struct(CELLS, CELLS, width)

    gathered_x = lax.all_to_all(
        jnp.broadcast_to(packed_x, (across_x, rows_y, rows_x * depth)), "gx", 0, 0, tiled=True
    )
    send_y, lines = call(
        functools.partial(start_kernel, depth, across_y),
        [struct(across_y, CELLS, 2 * width + LANES), block],
    )(cotangent, packed_y, inverse_rate)
    received_y = lax.all_to_all(send_y, "gy", 0, 0, tiled=True)
    rates, inverse_conc, net, back = call(
        functools.partial(rates_kernel, depth),
        [
            struct(reactions, rows_x * rows_y * depth),
            struct(species, rows_x * rows_y * depth),
            jax.ShapeDtypeStruct((reactions, 2 * species), jnp.bfloat16),
            jax.ShapeDtypeStruct((species, reactions), jnp.bfloat16),
        ],
        [turn],
    )(concentration, rate_constant[:, None], reactants, products)
    weight, forward, backward, gain = call(
        functools.partial(weights_kernel, depth, across_x, "gx"),
        [struct(across_x, CELLS, width), block, block, block],
        shots(across_x),
    )(gathered_x, inverse_rate)
    send_x, sources = call(
        functools.partial(middle_kernel, depth, across_y, "gy", across_x, "gx"),
        [struct(across_x, CELLS, width), block],
        [pltpu.VMEM((across_y, CELLS, LANES), jnp.float32)] + shots(across_y) + [turn],
    )(received_y, lines, inverse_rate, rates, inverse_conc, net, back, forward, backward)
    received_x = lax.all_to_all(send_x, "gx", 0, 0, tiled=True)
    return call(functools.partial(finish_kernel, across_x, "gx"), block)(
        received_x, weight, sources, forward, backward, gain
    )


def solution(mesh):
    placed = (P("gx", "gy", None), P("gx", "gy", None), P("gx", "gy", None), P(), P(), P(), P())
    return jax.shard_map(
        on_device, mesh=mesh, in_specs=placed, out_specs=P("gx", "gy", None), check_vma=False
    )
```

time: 108 us -> 86.5 us (0.80)
  the two profiles are of different devices: /device:TPU:64 before, /device:TPU:9 now
where the time goes in v1:
time: 86.5 us; the launch traced here: 85.9 us
  Pallas kernels  22.4 us (26%)
  starting transfers between devices  22.3 us (26%)
  blocking collectives  22.1 us (26%)
  waiting for transfers between devices  11.5 us (13%)
  local copies, waits for them, and re-layouts  7.52 us (9%)
    pallas_call x5, Pallas kernels, run(): pl.pallas_call(kernel, out_shape=out_shape, in_specs=[whole] * len(operan...  22.4 us
    all_to_all x1, blocking collectives, on_device(): received_x = lax.all_to_all(send_x, 'gx', 0, 0, tiled=True)  22.1 us
    all_to_all x1, starting transfers between devices, on_device(): received_y = lax.all_to_all(send_y, 'gy', 0, 0, tiled=True)  12.5 us
    all_to_all x1, starting transfers between devices, on_device(): lax.all_to_all(jnp.broadcast_to(packed_x, (across_x, rows_y, rows_x * dep...  9.74 us
    all_to_all x1, waiting for transfers between devices, on_device(): received_y = lax.all_to_all(send_y, 'gy', 0, 0, tiled=True)  6.09 us
    all_to_all x1, waiting for transfers between devices, on_device(): lax.all_to_all(jnp.broadcast_to(packed_x, (across_x, rows_y, rows_x * dep...  5.45 us
    unnamed x16, local copies, waits for them, and re-layouts  3.8 us
  transfers between devices with their start and end apart: 2, of which 2 were waited for; matrix products, arithmetic and copies ran while one was open for 4% of the time, Pallas kernels for 13%

profile of v1, /device:TPU:9, one launch (start us, length us, event | category | flops | bytes accessed | tf_op | source)
XLA Modules:
  0.0 85.9 jit_solution(16635070671964973461)
XLA Ops:
  0.0 0.8 copy.13
  0.8 0.1 reshape.7
  0.8 0.7 broadcast_in_dim.11
  1.5 0.0 copy-start.2
  1.5 9.7 %all-to-all-start.1 = ((f32[32,8,128]{2,1,0:T(8,128)}), f32[32,8,128]{2,1,0:T(8,128)S(1)}, u32[]{:S(2)}, u32[]{:S(2)}) async-start(f32[32,8,128]{2,1,0:T(8,128)} %broadcast_in_dim.11), calls=%async_computation.1 | async-start | bytes 262144 | tf_op jit(solution)/shard_map/all_to_all | solution.py:363
  11.3 0.0 copy-done.2
  11.3 0.0 copy-start.6
  11.3 0.7 reshape.6.cond_ref
  11.9 0.0 copy-done.6
  12.0 0.1 broadcast_in_dim.9
  12.0 0.7 broadcast_in_dim_reshape.3.inverse_ref
  12.7 1.9 %shard_map.73 = (f32[16,8,1152]{2,1,0:T(8,128)}, f32[8,8,512]{2,1,0:T(8,128)}) custom-call(f32[8,8,512]{2,1,0:T(8,128)} %cot_ref.1, f32[8,128]{1,0:T(8,128)} %reshape.6.cond_ref, f32[1,512]{1,0:T(1,128)} %broadcast_in_dim_reshape.3.inverse_ref), custom_call_target="tpu_custom_call" | custom-call | tf_op jit(solution)/shard_map/pallas_call | solution.py:20
  14.6 5.4 %all-to-all-done.1.gathered_ref = f32[32,8,128]{2,1,0:T(8,128)S(1)} async-done(((f32[32,8,128]{2,1,0:T(8,128)}), f32[32,8,128]{2,1,0:T(8,128)S(1)}, u32[]{:S(2)}, u32[]{:S(2)}) %all-to-all-start.1) | async-done | bytes 131104 | tf_op jit(solution)/shard_map/all_to_all | solution.py:363
  20.1 0.0 copy-start.1
  20.1 0.7 copy-done.1
  20.7 12.5 %all-to-all-start = ((f32[16,8,1152]{2,1,0:T(8,128)}), f32[16,8,1152]{2,1,0:T(8,128)S(1)}, u32[]{:S(2)}, u32[]{:S(2)}) async-start(f32[16,8,1152]{2,1,0:T(8,128)} %get-tuple-element.17), calls=%async_computation | async-start | bytes 1179648 | tf_op jit(solution)/shard_map/all_to_all | solution.py:370
  33.3 0.0 copy-start.5
  33.3 0.7 copy-done.5
  33.9 0.0 copy-start.3
  33.9 0.8 copy.10.rate_ref
  34.7 0.0 copy-done.3
  34.7 0.0 copy-start.4
  34.7 0.8 copy.11.reactants_ref
  35.5 0.0 copy-done.4
  35.5 0.8 copy.12.products_ref
  36.3 2.7 %shard_map.74 = (f32[256,1024]{1,0:T(8,128)}, f32[32,1024]{1,0:T(8,128)}, bf16[256,64]{1,0:T(8,128)(2,1)}, bf16[32,256]{1,0:T(8,128)(2,1)}) custom-call(f32[8,8,512]{2,1,0:T(8,128)} %conc_ref.1, f32[256,1]{1,0:T(8,128)} %copy.10.rate_ref, s32[256,2]{1,0:T(8,128)} %copy.11.reactants_ref, s32[256,2]{1,0:T(8,128)} %copy.12.products_ref), custom_call_target="tpu_custom_call" | custom-call | tf_op jit(solution)/shard_map/pallas_call | solution.py:20
  39.0 6.7 %shard_map.75 = (f32[32,8,512]{2,1,0:T(8,128)}, f32[8,8,512]{2,1,0:T(8,128)}, f32[8,8,512]{2,1,0:T(8,128)}, f32[8,8,512]{2,1,0:T(8,128)}) custom-call(f32[32,8,128]{2,1,0:T(8,128)} %copy-done.1, f32[1,512]{1,0:T(1,128)} %broadcast_in_dim_reshape.3.inverse_ref), custom_call_target="tpu_custom_call" | custom-call | tf_op jit(solution)/shard_map/pallas_call | solution.py:20
  45.7 6.1 %all-to-all-done.received_ref = f32[16,8,1152]{2,1,0:T(8,128)S(1)} async-done(((f32[16,8,1152]{2,1,0:T(8,128)}), f32[16,8,1152]{2,1,0:T(8,128)S(1)}, u32[]{:S(2)}, u32[]{:S(2)}) %all-to-all-start) | async-done | bytes 589856 | tf_op jit(solution)/shard_map/all_to_all | solution.py:370
  51.8 0.9 copy-done
  52.7 8.9 %shard_map.76 = (f32[32,8,512]{2,1,0:T(8,128)}, f32[8,8,512]{2,1,0:T(8,128)}) custom-call(f32[16,8,1152]{2,1,0:T(8,128)} %copy-done, f32[8,8,512]{2,1,0:T(8,128)} %get-tuple-element.18.lines_ref, f32[1,512]{1,0:T(1,128)} %broadcast_in_dim_reshape.3.inverse_ref, f32[256,1024]{1,0:T(8,128)} %get-tuple-element.19.rates_ref, ...), custom_call_target="tpu_custom_call" | custom-call | tf_op jit(solution)/shard_map/pallas_call | solution.py:20
  61.6 22.1 %all_to_all.15.received_ref = f32[32,8,512]{2,1,0:T(8,128)} all-to-all(f32[32,8,512]{2,1,0:T(8,128)} %get-tuple-element.25), channel_id=1, replica_groups=mesh['gx'=32,'gy'=16] {'gx'}, dimensions={0} | all-to-all | bytes 1048576 | tf_op jit(solution)/shard_map/all_to_all | solution.py:391
  83.7 2.2 %shard_map.77 = f32[8,8,512]{2,1,0:T(8,128)} custom-call(f32[32,8,512]{2,1,0:T(8,128)} %all_to_all.15.received_ref, f32[32,8,512]{2,1,0:T(8,128)} %get-tuple-element.26.weight_ref, f32[8,8,512]{2,1,0:T(8,128)} %get-tuple-element.27.sources_ref, f32[8,8,512]{2,1,0:T(8,128)} %get-tuple-element.23.forward_ref, f32[8,8,512]{2,1,0:T(8,128)} %get-tuple-element.24.backward_ref, ...), custom_call_target="tpu_custom_call" | custom-call | tf_op jit(solution)/shard_map/pallas_call | solution.py:20
  (2 shorter events, 0.0 us)
Async XLA Ops:
  1.5 9.8 %copy-start.2 = (f32[8,8,16]{2,1,0:T(8,128)S(1)}, f32[8,8,16]{2,1,0:T(8,128)}, u32[]{:S(2)}) copy-start(f32[8,8,16]{2,1,0:T(8,128)} %param.9) | copy-start | bytes 12292
  1.5 18.6 %all-to-all-start.1 = ((f32[32,8,128]{2,1,0:T(8,128)}), f32[32,8,128]{2,1,0:T(8,128)S(1)}, u32[]{:S(2)}, u32[]{:S(2)}) async-start(f32[32,8,128]{2,1,0:T(8,128)} %broadcast_in_dim.11), calls=%async_computation.1 | async-start | bytes 262144 | tf_op jit(solution)/shard_map/all_to_all | solution.py:363
  11.3 0.7 copy-start.6
  20.1 0.7 copy-start.1
  20.7 31.1 %all-to-all-start = ((f32[16,8,1152]{2,1,0:T(8,128)}), f32[16,8,1152]{2,1,0:T(8,128)S(1)}, u32[]{:S(2)}, u32[]{:S(2)}) async-start(f32[16,8,1152]{2,1,0:T(8,128)} %get-tuple-element.17), calls=%async_computation | async-start | bytes 1179648 | tf_op jit(solution)/shard_map/all_to_all | solution.py:370
  33.3 0.7 copy-start.5
  33.9 0.8 copy-start.3
  34.7 0.8 copy-start.4
  51.8 0.9 copy-start

commit v2 on v1

v2 whole, which is shorter than its diff:
```python
import functools

import jax
import jax.numpy as jnp
from jax import lax
from jax.experimental import pallas as pl
from jax.experimental.pallas import tpu as pltpu
from jax.sharding import PartitionSpec as P


CELLS = 8
LANES = 128
ROWS = 8
LIMIT = 16 << 20


def call(kernel, out_shape, scratch_shapes=()):
    whole = pl.BlockSpec(memory_space=pltpu.VMEM)

    def run(*operands):
        outs = jax.tree.map(lambda _: whole, out_shape)
        return pl.pallas_call(
            kernel,
            out_shape=out_shape,
            in_specs=[whole] * len(operands),
            out_specs=outs,
            scratch_shapes=list(scratch_shapes),
            compiler_params=pltpu.CompilerParams(vmem_limit_bytes=LIMIT),
        )(*operands)

    return run


def struct(*shape):
    return jax.ShapeDtypeStruct(shape, jnp.float32)


def cell_rates(cond, diffusivity, width, depth):
    lane = lax.broadcasted_iota(jnp.int32, (depth, width), 1)
    same_depth = lax.rem(lane, depth) == lax.broadcasted_iota(jnp.int32, (depth, width), 0)
    species = width // depth
    lane = lax.broadcasted_iota(jnp.int32, (species, width), 1)
    same_species = lax.div(lane, depth) == lax.broadcasted_iota(jnp.int32, (species, width), 0)
    highest = lax.Precision.HIGHEST
    spread = jnp.dot(
        (1.0 / cond).reshape(-1, depth),
        same_depth.astype(jnp.float32),
        precision=highest,
        preferred_element_type=jnp.float32,
    )
    scale = jnp.dot(
        jnp.broadcast_to(1.0 / diffusivity, (CELLS, species)),
        same_species.astype(jnp.float32),
        precision=highest,
        preferred_element_type=jnp.float32,
    )
    tiles = spread.reshape(CELLS, CELLS, width)
    return [tiles[cell] * scale for cell in range(CELLS)]


def factors(rates):
    one = jnp.ones_like(rates[0])
    zero = jnp.zeros_like(one)

    def shoot(value, step, order):
        values = {}
        for cell in order:
            values[cell] = value
            step = step + rates[cell] * value
            value = value + step
        return values, value, step

    flat, flat_out, flat_step = shoot(one, zero, range(CELLS))
    slope, slope_out, slope_step = shoot(zero, one, range(CELLS))
    right, _, _ = shoot(one, one, reversed(range(CELLS)))
    inverse = 1.0 / (flat_out + slope_out)
    to_last = [(flat[k] + slope[k]) * inverse for k in range(CELLS)]
    to_first = [right[k] * inverse for k in range(CELLS)]
    transfer = (flat_step, slope_step, flat[CELLS - 1], slope[CELLS - 1])
    return to_first, to_last, transfer


def local_solution(sources, rates, to_first, to_last):
    first, last = to_first[0] * 0.0, None
    before, after = [None] * CELLS, [None] * CELLS
    running = first
    for k in range(CELLS):
        before[k] = running
        if k < CELLS - 1:
            running = (to_last[k] / to_last[k + 1]) * (sources[k] + running)
    running = first
    for k in reversed(range(CELLS)):
        after[k] = running
        if k > 0:
            running = (to_first[k] / to_first[k - 1]) * (sources[k] + running)
    return [
        (sources[k] + before[k] + after[k]) * (to_first[k] * to_last[k] / to_first[CELLS - 1])
        for k in range(CELLS)
    ]


def total(weights, sources):
    terms = [weight * source for weight, source in zip(weights, sources, strict=True)]
    while len(terms) > 1:
        terms = [a + b for a, b in zip(terms[::2], terms[1::2], strict=True)]
    return terms[0]


def put_rows(send_ref, rows):
    for row, value in enumerate(rows):
        for tile in range(value.shape[1] // LANES):
            send_ref[pl.ds(tile * ROWS + row, CELLS, stride=CELLS * 4), :] = value[
                :, tile * LANES : (tile + 1) * LANES
            ]


def get_ends(back_ref):
    return [
        jnp.concatenate(
            [back_ref[pl.ds(tile * 2 + side, CELLS, stride=CELLS), :] for tile in range(4)], axis=1
        )
        for side in range(2)
    ]


def start_kernel(depth, cot_ref, cond_ref, diffusivity_ref, send_ref):
    width = cot_ref.shape[2]
    lines = jnp.swapaxes(cot_ref[...], 0, 1)
    cond = jnp.swapaxes(cond_ref[...], 0, 1)
    sources = [lines[cell] for cell in range(CELLS)]
    rates = cell_rates(cond, diffusivity_ref[...], width, depth)
    to_first, to_last, transfer = factors(rates)
    blank = jnp.zeros_like(rates[0])
    put_rows(
        send_ref,
        [total(to_first, sources), total(to_last, sources), *transfer, blank, blank],
    )


def solve_kernel(blocks, tiles, got_ref, out_ref, *scratch):
    value_l, step_l, value_r, step_r, ratio_l, add_l, ratio_r, add_r, sum_l, sum_r = scratch
    one = jnp.ones((1, LANES), jnp.float32)

    def pick(block, tile, row):
        return got_ref[pl.ds((block * tiles + tile) * ROWS + row, 1), :]

    def whole(tile, row):
        return got_ref[pl.ds(tile * ROWS + row, blocks, stride=ROWS * tiles), :]

    for tile in range(tiles):
        left, left_step, right, right_step = one, one, one, one
        for block in range(blocks):
            mirror = blocks - 1 - block
            value_l[tile, pl.ds(block, 1), :] = left
            step_l[tile, pl.ds(block, 1), :] = left_step
            value_r[tile, pl.ds(mirror + 1, 1), :] = right
            step_r[tile, pl.ds(mirror + 1, 1), :] = right_step
            c, d, e, f = (pick(block, tile, row) for row in range(2, 6))
            kept = e * left + f * left_step
            left_step = c * left + d * left_step
            left = kept + left_step
            c, d, e, f = (pick(mirror, tile, row) for row in range(2, 6))
            kept = d * right + f * right_step
            right_step = c * right + e * right_step
            right = kept + right_step
        value_l[tile, pl.ds(blocks, 1), :] = left
        step_l[tile, pl.ds(blocks, 1), :] = left_step
        value_r[tile, pl.ds(0, 1), :] = right
        step_r[tile, pl.ds(0, 1), :] = right_step
    for tile in range(tiles):
        near = pl.ds(0, blocks)
        far = pl.ds(1, blocks)
        first, last = whole(tile, 0), whole(tile, 1)
        inverse = 1.0 / value_l[tile, far, :]
        at = value_l[tile, near, :]
        ratio_l[tile] = at * inverse
        add_l[tile] = last + (at - step_l[tile, near, :]) * inverse * first
        inverse = 1.0 / value_r[tile, near, :]
        at = value_r[tile, far, :]
        ratio_r[tile] = at * inverse
        add_r[tile] = first + (at - step_r[tile, far, :]) * inverse * last
    for tile in range(tiles):
        left = jnp.zeros_like(one)
        right = jnp.zeros_like(one)
        for block in range(blocks):
            mirror = blocks - 1 - block
            sum_l[tile, pl.ds(block, 1), :] = left
            sum_r[tile, pl.ds(mirror + 1, 1), :] = right
            here, there = pl.ds(block, 1), pl.ds(mirror, 1)
            left = ratio_l[tile, here, :] * left + add_l[tile, here, :]
            right = ratio_r[tile, there, :] * right + add_r[tile, there, :]
        sum_l[tile, pl.ds(blocks, 1), :] = left
        sum_r[tile, pl.ds(0, 1), :] = right
    for tile in range(tiles):
        for side in range(2):
            rows = pl.ds(side, blocks)
            gap_l = step_l[tile, rows, :] / value_l[tile, rows, :]
            gap_r = step_r[tile, rows, :] / value_r[tile, rows, :]
            inverse = 1.0 / (gap_l + gap_r * (1.0 - gap_l))
            left, right = sum_l[tile, rows, :], sum_r[tile, rows, :]
            if side == 0:
                ends = (left + (1.0 - gap_l) * right) * inverse
            else:
                ends = (right + (1.0 - gap_r) * left) * inverse
            out_ref[pl.ds(tile * 2 + side, blocks, stride=2 * tiles), :] = ends


def to_species(cells, turn_ref, depth):
    rows = cells.shape[0]
    turn_ref[...] = jnp.concatenate([cells, cells], axis=0).T
    species = cells.shape[1] // depth
    low = lax.broadcasted_iota(jnp.int32, (species, 2 * rows), 1) < rows
    pairs = []
    for pair in range(depth // 2):
        even = turn_ref[pl.ds(2 * pair, species, stride=depth), :]
        odd = turn_ref[pl.ds(2 * pair + 1, species, stride=depth), :]
        pairs.append(jnp.where(low, even, odd))
    return pairs


def from_species(pairs, turn_ref, depth):
    species, columns = pairs[0].shape
    for pair, tile in enumerate(pairs):
        turn_ref[pl.ds(2 * pair, species, stride=depth), :] = tile
        turn_ref[pl.ds(2 * pair + 1, species, stride=depth), :] = pltpu.roll(
            tile, columns // 2, 1
        )
    return turn_ref[...].T[: columns // 2]


def halves(value):
    high = value.astype(jnp.bfloat16)
    return high, (value - high.astype(jnp.float32)).astype(jnp.bfloat16)


def counts(pair_ref, species):
    ids = lax.broadcasted_iota(jnp.int32, (pair_ref.shape[0], species), 1)
    return (pair_ref[:, 0:1] == ids).astype(jnp.float32) + (pair_ref[:, 1:2] == ids).astype(
        jnp.float32
    )


def counts(pair_ref, species):
    ids = lax.broadcasted_iota(jnp.int32, (species, pair_ref.shape[1]), 0)
    return (pair_ref[0:1, :] == ids).astype(jnp.float32) + (pair_ref[1:2, :] == ids).astype(
        jnp.float32
    )


def prepare_kernel(
    depth, cot_ref, conc_ref, cond_ref, diffusivity_ref, rate_ref, reactants_ref, products_ref,
    rates_ref, inverse_ref, net_ref, back_ref, local_y_ref, first_y_ref, last_y_ref, first_x_ref,
    last_x_ref, transfer_ref, turn_ref,
):
    rows_x, rows_y, width = conc_ref.shape
    species = width // depth
    used = counts(reactants_ref, species)
    net = counts(products_ref, species) - used
    back_ref[...] = used.astype(jnp.bfloat16)
    net_ref[...] = jnp.concatenate([net, net], axis=0).T.astype(jnp.bfloat16)
    twice = jnp.concatenate([used, used], axis=0).T.astype(jnp.bfloat16)
    constant = jnp.broadcast_to(rate_ref[...], (LANES, rate_ref.shape[1])).T
    pairs = to_species(conc_ref[...].reshape(rows_x * rows_y, width), turn_ref, depth)
    for pair, conc in enumerate(pairs):
        columns = pl.ds(pair * conc.shape[1], conc.shape[1])
        inverse_ref[:, columns] = 1.0 / conc
        stacked = jnp.concatenate(halves(jnp.log(conc)), axis=0)
        exponent = jnp.dot(twice, stacked, preferred_element_type=jnp.float32)
        rates_ref[:, columns] = constant * jnp.exp(exponent)

    cond = cond_ref[...]
    rates = cell_rates(cond, diffusivity_ref[...], width, depth)
    to_first, to_last, transfer = factors(rates)
    for k in range(CELLS):
        first_x_ref[k] = to_first[k]
        last_x_ref[k] = to_last[k]
    for k in range(4):
        transfer_ref[k] = transfer[k]
    rates = cell_rates(jnp.swapaxes(cond, 0, 1), diffusivity_ref[...], width, depth)
    to_first, to_last, _ = factors(rates)
    lines = jnp.swapaxes(cot_ref[...], 0, 1)
    local = local_solution([lines[k] for k in range(CELLS)], rates, to_first, to_last)
    for k in range(CELLS):
        local_y_ref[k] = local[k] * rates[k]
        first_y_ref[k] = to_first[k] * rates[k]
        last_y_ref[k] = to_last[k] * rates[k]


def chemistry(field, rates, inverse, net, back):
    def transposed(vector):
        stacked = jnp.concatenate(halves(vector), axis=0)
        flows = jnp.dot(net, stacked, preferred_element_type=jnp.float32) * rates
        high, low = halves(flows)
        gathered = jnp.dot(back, high, preferred_element_type=jnp.float32) + jnp.dot(
            back, low, preferred_element_type=jnp.float32
        )
        return gathered * inverse

    third = field + transposed(field) * (1.0 / 3.0)
    second = field + transposed(third) * 0.5
    return field + transposed(second)


def middle_kernel(
    depth, ends_ref, local_ref, first_ref, last_ref, rates_ref, inverse_ref, net_ref, back_ref,
    first_x_ref, last_x_ref, transfer_ref, send_ref, sources_ref, turn_ref,
):
    width = local_ref.shape[2]
    left, right = get_ends(ends_ref)
    solved = jnp.stack(
        [local_ref[k] + first_ref[k] * left + last_ref[k] * right for k in range(CELLS)], axis=0
    )
    solved = jnp.swapaxes(solved, 0, 1).reshape(CELLS * CELLS, width)
    net = net_ref[...]
    back = back_ref[...]
    pairs = to_species(solved, turn_ref, depth)
    columns = pairs[0].shape[1]
    done = []
    for chunk in range(len(pairs) // 2):
        at = pl.ds(chunk * 2 * columns, 2 * columns)
        field = jnp.concatenate(pairs[2 * chunk : 2 * chunk + 2], axis=1)
        result = chemistry(field, rates_ref[:, at], inverse_ref[:, at], net, back)
        done += [result[:, :columns], result[:, columns:]]
    changed = from_species(done, turn_ref, depth).reshape(CELLS, CELLS, width)
    sources_ref[...] = changed
    sources = [changed[k] for k in range(CELLS)]
    blank = jnp.zeros_like(left)
    put_rows(
        send_ref,
        [
            total([first_x_ref[k] for k in range(CELLS)], sources),
            total([last_x_ref[k] for k in range(CELLS)], sources),
            *(transfer_ref[k] for k in range(4)),
            blank,
            blank,
        ],
    )


def finish_kernel(
    depth, ends_ref, cond_ref, diffusivity_ref, sources_ref, first_ref, last_ref, out_ref
):
    width = out_ref.shape[2]
    rates = cell_rates(cond_ref[...], diffusivity_ref[...], width, depth)
    to_first = [first_ref[k] for k in range(CELLS)]
    to_last = [last_ref[k] for k in range(CELLS)]
    local = local_solution([sources_ref[k] for k in range(CELLS)], rates, to_first, to_last)
    left, right = get_ends(ends_ref)
    for k in range(CELLS):
        out_ref[k] = (local[k] + to_first[k] * left + to_last[k] * right) * rates[k]


def exchange(rows, axis):
    members = lax.axis_size(axis)
    blocks = rows.reshape(members, rows.shape[0] // members, LANES)
    return lax.all_to_all(blocks, axis, 0, 0, tiled=True).reshape(rows.shape)


def solve_lines(send, axis):
    blocks = lax.axis_size(axis)
    tiles = send.shape[0] // (blocks * ROWS)
    states = pltpu.VMEM((tiles, blocks + CELLS, LANES), jnp.float32)
    terms = pltpu.VMEM((tiles, blocks, LANES), jnp.float32)
    ends = call(
        functools.partial(solve_kernel, blocks, tiles),
        struct(2 * blocks * tiles, LANES),
        [states] * 4 + [terms] * 4 + [states] * 2,
    )(exchange(send, axis))
    return exchange(ends, axis)


def on_device(
    cotangent, concentration, conductance, diffusivity, rate_constant, reactants, products
):
    rows_x, rows_y, width = cotangent.shape
    depth = conductance.shape[2]
    species = diffusivity.shape[0]
    reactions = rate_constant.shape[0]
    columns = rows_x * rows_y * depth
    diffusivity = diffusivity[None, :]
    turn = pltpu.VMEM((width, 2 * rows_x * rows_y), jnp.float32)
    block = struct(CELLS, CELLS, width)
    send = struct(CELLS * (width // LANES) * ROWS, LANES)

    send_y = call(functools.partial(start_kernel, depth), send)(
        cotangent, conductance, diffusivity
    )
    rates, inverse, net, back, local_y, first_y, last_y, first_x, last_x, transfer = call(
        functools.partial(prepare_kernel, depth),
        [
            struct(reactions, columns),
            struct(species, columns),
            jax.ShapeDtypeStruct((reactions, 2 * species), jnp.bfloat16),
            jax.ShapeDtypeStruct((species, reactions), jnp.bfloat16),
            block,
            block,
            block,
            block,
            block,
            struct(4, CELLS, width),
        ],
        [turn],
    )(
        cotangent,
        concentration,
        conductance,
        diffusivity,
        rate_constant[None, :],
        reactants.T,
        products.T,
    )
    ends_y = solve_lines(send_y, "gy")
    send_x, sources = call(functools.partial(middle_kernel, depth), [send, block], [turn])(
        ends_y, local_y, first_y, last_y, rates, inverse, net, back, first_x, last_x, transfer
    )
    ends_x = solve_lines(send_x, "gx")
    return call(functools.partial(finish_kernel, depth), block)(
        ends_x, conductance, diffusivity, sources, first_x, last_x
    )


def solution(mesh):
    placed = (P("gx", "gy", None), P("gx", "gy", None), P("gx", "gy", None), P(), P(), P(), P())
    return jax.shard_map(
        on_device, mesh=mesh, in_specs=placed, out_specs=P("gx", "gy", None), check_vma=False
    )
```

time: 86.5 us -> 72 us (0.83)
  the two profiles are of different devices: /device:TPU:9 before, /device:TPU:8 now
where the time goes in v2:
time: 72 us; the launch traced here: 71.6 us
  blocking collectives  51.9 us (72%)
  Pallas kernels  6.91 us (10%)
  waiting for transfers between devices  6.04 us (8%)
  starting transfers between devices  3.63 us (5%)
  local copies, waits for them, and re-layouts  2.99 us (4%)
    all_to_all x3, blocking collectives, exchange(): return lax.all_to_all(blocks, axis, 0, 0, tiled=True).reshape(rows.shape)  51.9 us
    pallas_call x6, Pallas kernels, run(): pl.pallas_call(kernel, out_shape=out_shape, in_specs=[whole] * len(operan...  6.91 us
    all_to_all x1, waiting for transfers between devices, exchange(): return lax.all_to_all(blocks, axis, 0, 0, tiled=True).reshape(rows.shape)  6.04 us
    all_to_all x1, starting transfers between devices, exchange(): return lax.all_to_all(blocks, axis, 0, 0, tiled=True).reshape(rows.shape)  3.63 us
    unnamed x18, local copies, waits for them, and re-layouts  2.99 us
  transfers between devices with their start and end apart: 1, of which 1 were waited for; matrix products, arithmetic and copies ran while one was open for 0% of the time, Pallas kernels for 1%

profile of v2, /device:TPU:8, one launch (start us, length us, event | category | flops | bytes accessed | tf_op | source)
XLA Modules:
  0.0 71.6 jit_solution(2379174434448348402)
XLA Ops:
  0.0 0.0 copy-start.5
  0.0 0.7 copy-done.5
  0.7 0.0 copy-start
  0.7 0.9 %copy-done = f32[8,8,512]{2,1,0:T(8,128)S(1)} copy-done((f32[8,8,512]{2,1,0:T(8,128)S(1)}, f32[8,8,512]{2,1,0:T(8,128)}, u32[]{:S(2)}) %copy-start) | copy-done | bytes 131096
  1.6 0.0 copy-start.2
  1.6 0.8 %copy-done.2 = f32[8,8,16]{2,1,0:T(8,128)S(1)} copy-done((f32[8,8,16]{2,1,0:T(8,128)S(1)}, f32[8,8,16]{2,1,0:T(8,128)}, u32[]{:S(2)}) %copy-start.2) | copy-done | bytes 4120
  2.3 0.4 shard_map.73
  2.7 0.0 copy-start.4
  2.7 19.0 %all_to_all.20 = f32[16,16,128]{2,1,0:T(8,128)S(1)} all-to-all(f32[16,16,128]{2,1,0:T(8,128)S(1)} %bitcast.14), channel_id=1, replica_groups=mesh['gx'=32,'gy'=16] {'gy'}, dimensions={0} | all-to-all | bytes 262144 | tf_op jit(solution)/shard_map/all_to_all | solution.py:356
  21.7 0.0 copy-start.1
  21.7 0.8 %shard_map.74 = f32[64,128]{1,0:T(8,128)} custom-call(f32[256,128]{1,0:T(8,128)S(1)} %bitcast.12), custom_call_target="tpu_custom_call" | custom-call | tf_op jit(solution)/shard_map/pallas_call | solution.py:22
  22.5 0.0 copy-start.3
  22.5 3.6 %all-to-all-start.1 = ((f32[16,4,128]{2,1,0:T(4,128)}), f32[16,4,128]{2,1,0:T(4,128)S(1)}, u32[]{:S(2)}, u32[]{:S(2)}) async-start(f32[16,4,128]{2,1,0:T(4,128)} %bitcast.3), calls=%async_computation.1 | async-start | bytes 65536 | tf_op jit(solution)/shard_map/all_to_all | solution.py:356
  26.1 0.0 copy-start.7
  26.1 0.0 copy-start.6
  26.2 0.0 copy-start.8
  26.2 0.0 copy-done.4
  26.2 0.0 copy-done.1
  26.2 0.0 copy-done.3
  26.2 0.6 copy-done.7
  26.8 0.0 copy-done.6
  26.8 0.0 copy-done.8
  26.8 0.9 %shard_map.75 = (f32[256,1024]{1,0:T(8,128)S(1)}, f32[32,1024]{1,0:T(8,128)S(1)}, bf16[256,64]{1,0:T(8,128)(2,1)S(1)}, bf16[32,256]{1,0:T(8,128)(2,1)S(1)}, f32[...) custom-call(f32[8,8,512]{2,1,0:T(8,128)S(1)} %copy-done.1, ...), custom_call_target="tpu_custom_call" | custom-call | tf_op jit(solution)/shard_map/pallas_call | solution.py:22
  27.7 6.0 %all-to-all-done.1 = f32[16,4,128]{2,1,0:T(4,128)S(1)} async-done(((f32[16,4,128]{2,1,0:T(4,128)}), f32[16,4,128]{2,1,0:T(4,128)S(1)}, u32[]{:S(2)}, u32[]{:S(2)}) %all-to-all-start.1) | async-done | bytes 32800 | tf_op jit(solution)/shard_map/all_to_all | solution.py:356
  33.8 3.7 %shard_map.76 = (f32[256,128]{1,0:T(8,128)S(1)}, f32[8,8,512]{2,1,0:T(8,128)S(1)}) custom-call(f32[64,128]{1,0:T(8,128)S(1)} %bitcast.15, f32[8,8,512]{2,1,0:T(8,128)S(1)} %get-tuple-element.17.local_ref, f32[8,8,512]{2,1,0:T(8,128)S(1)} %get-tuple-element.18.first_ref, f32[8,8,512]{2,1,0:T(8,128)S(1)} %get-tuple-element.19.last_ref, ...), custom_call_target="tpu_custom_call" | custom-call | tf_op jit(solution)/shard_map/pallas_call | solution.py:22
  37.5 20.0 %all_to_all.21 = f32[32,8,128]{2,1,0:T(8,128)S(1)} all-to-all(f32[32,8,128]{2,1,0:T(8,128)S(1)} %bitcast.17), channel_id=1, replica_groups=mesh['gx'=32,'gy'=16] {'gx'}, dimensions={0} | all-to-all | bytes 262144 | tf_op jit(solution)/shard_map/all_to_all | solution.py:356
  57.5 0.2 shard_map.77
  57.7 13.0 %all_to_all.22 = f32[32,2,128]{2,1,0:T(2,128)S(1)} all-to-all(f32[32,2,128]{2,1,0:T(2,128)S(1)} %bitcast.16), channel_id=1, replica_groups=mesh['gx'=32,'gy'=16] {'gx'}, dimensions={0} | all-to-all | bytes 65536 | tf_op jit(solution)/shard_map/all_to_all | solution.py:356
  70.6 0.9 %shard_map.78 = f32[8,8,512]{2,1,0:T(8,128)} custom-call(f32[64,128]{1,0:T(8,128)S(1)} %bitcast.18, f32[8,8,16]{2,1,0:T(8,128)S(1)} %copy-done.3, f32[1,32]{1,0:T(1,128)S(1)} %bitcast.21, f32[8,8,512]{2,1,0:T(8,128)S(1)} %get-tuple-element.28.sources_ref, f32[8,8,512]{2,1,0:T(8,128)S(1)} %get-tuple-element.24.first_x_ref.first_ref, ...), custom_call_target="tpu_custom_call" | custom-call | tf_op jit(solution)/shard_map/pallas_call | solution.py:22
Async XLA Ops:
  0.0 0.7 copy-start.5
  0.7 0.9 %copy-start = (f32[8,8,512]{2,1,0:T(8,128)S(1)}, f32[8,8,512]{2,1,0:T(8,128)}, u32[]{:S(2)}) copy-start(f32[8,8,512]{2,1,0:T(8,128)} %cot_ref.3) | copy-start | bytes 393220
  1.6 0.8 %copy-start.2 = (f32[8,8,16]{2,1,0:T(8,128)S(1)}, f32[8,8,16]{2,1,0:T(8,128)}, u32[]{:S(2)}) copy-start(f32[8,8,16]{2,1,0:T(8,128)} %cond_ref.5) | copy-start | bytes 12292
  2.7 23.4 %copy-start.4 = (f32[8,8,512]{2,1,0:T(8,128)S(1)}, f32[8,8,512]{2,1,0:T(8,128)}, u32[]{:S(2)}) copy-start(f32[8,8,512]{2,1,0:T(8,128)} %conc_ref.1) | copy-start | bytes 393220
  21.7 4.4 %copy-start.1 = (f32[8,8,512]{2,1,0:T(8,128)S(1)}, f32[8,8,512]{2,1,0:T(8,128)}, u32[]{:S(2)}) copy-start(f32[8,8,512]{2,1,0:T(8,128)} %cot_ref.3) | copy-start | bytes 393220
  22.5 3.7 %copy-start.3 = (f32[8,8,16]{2,1,0:T(8,128)S(1)}, f32[8,8,16]{2,1,0:T(8,128)}, u32[]{:S(2)}) copy-start(f32[8,8,16]{2,1,0:T(8,128)} %cond_ref.5) | copy-start | bytes 12292
  22.5 11.3 %all-to-all-start.1 = ((f32[16,4,128]{2,1,0:T(4,128)}), f32[16,4,128]{2,1,0:T(4,128)S(1)}, u32[]{:S(2)}, u32[]{:S(2)}) async-start(f32[16,4,128]{2,1,0:T(4,128)} %bitcast.3), calls=%async_computation.1 | async-start | bytes 65536 | tf_op jit(solution)/shard_map/all_to_all | solution.py:356
  26.1 0.7 copy-start.7
  26.1 0.7 copy-start.6
  26.2 0.7 copy-start.8

commit v3 on v2

--- a/solution.py
+++ b/solution.py
@@ -14,15 +14,22 @@
 LIMIT = 16 << 20
 
 
-def call(kernel, out_shape, scratch_shapes=()):
-    whole = pl.BlockSpec(memory_space=pltpu.VMEM)
+def call(kernel, out_shape, scratch_shapes=(), far_in=(), far_out=()):
+    near = pl.BlockSpec(memory_space=pltpu.VMEM)
+    far = pl.BlockSpec(memory_space=pltpu.HBM)
 
     def run(*operands):
-        outs = jax.tree.map(lambda _: whole, out_shape)
+        operands = [
+            pltpu.with_memory_space_constraint(x, pltpu.HBM) if k in far_in else x
+            for k, x in enumerate(operands)
+        ]
+        outs = near
+        if isinstance(out_shape, list):
+            outs = [far if k in far_out else near for k in range(len(out_shape))]
         return pl.pallas_call(
             kernel,
             out_shape=out_shape,
-            in_specs=[whole] * len(operands),
+            in_specs=[far if k in far_in else near for k in range(len(operands))],
             out_specs=outs,
             scratch_shapes=list(scratch_shapes),
             compiler_params=pltpu.CompilerParams(vmem_limit_bytes=LIMIT),
@@ -80,23 +87,26 @@
     return to_first, to_last, transfer
 
 
-def local_solution(sources, rates, to_first, to_last):
-    first, last = to_first[0] * 0.0, None
+def sweep_factors(to_first, to_last):
+    ratio = to_last[0] * 0.0
+    forward = [to_last[k] / to_last[k + 1] for k in range(CELLS - 1)] + [ratio]
+    backward = [ratio] + [to_first[k] / to_first[k - 1] for k in range(1, CELLS)]
+    scale = 1.0 / to_first[CELLS - 1]
+    gains = [to_first[k] * to_last[k] * scale for k in range(CELLS)]
+    return forward, backward, gains
+
+
+def local_solution(sources, forward, backward, gains):
     before, after = [None] * CELLS, [None] * CELLS
-    running = first
+    running = sources[0] * 0.0
     for k in range(CELLS):
-        before[k] = running
-        if k < CELLS - 1:
-            running = (to_last[k] / to_last[k + 1]) * (sources[k] + running)
-    running = first
+        before[k] = sources[k] + running
+        running = forward[k] * before[k]
+    running = sources[0] * 0.0
     for k in reversed(range(CELLS)):
         after[k] = running
-        if k > 0:
-            running = (to_first[k] / to_first[k - 1]) * (sources[k] + running)
-    return [
-        (sources[k] + before[k] + after[k]) * (to_first[k] * to_last[k] / to_first[CELLS - 1])
-        for k in range(CELLS)
-    ]
+        running = backward[k] * (sources[k] + running)
+    return [(before[k] + after[k]) * gains[k] for k in range(CELLS)]
 
 
 def total(weights, sources):
@@ -123,8 +133,19 @@
     ]
 
 
-def start_kernel(depth, cot_ref, cond_ref, diffusivity_ref, send_ref):
+def start_kernel(
+    depth, cot_from, cond_from, diffusivity_from, send_ref, cot_ref, cond_ref, diffusivity_ref, sem
+):
     width = cot_ref.shape[2]
+    copies = [
+        pltpu.make_async_copy(cond_from, cond_ref, sem.at[0]),
+        pltpu.make_async_copy(diffusivity_from, diffusivity_ref, sem.at[1]),
+        pltpu.make_async_copy(cot_from, cot_ref, sem.at[2]),
+    ]
+    for copy in copies:
+        copy.start()
+    for copy in copies:
+        copy.wait()
     lines = jnp.swapaxes(cot_ref[...], 0, 1)
     cond = jnp.swapaxes(cond_ref[...], 0, 1)
     sources = [lines[cell] for cell in range(CELLS)]
@@ -249,15 +270,18 @@
 
 def prepare_kernel(
     depth, cot_ref, conc_ref, cond_ref, diffusivity_ref, rate_ref, reactants_ref, products_ref,
-    rates_ref, inverse_ref, net_ref, back_ref, local_y_ref, first_y_ref, last_y_ref, first_x_ref,
-    last_x_ref, transfer_ref, turn_ref,
+    jacobian_to, inverse_ref, local_y_ref, ends_y_ref, ends_x_ref, sweep_x_ref, transfer_ref,
+    turn_ref, rates_ref, pairs_ref, jacobian_ref, sem,
 ):
     rows_x, rows_y, width = conc_ref.shape
     species = width // depth
     used = counts(reactants_ref, species)
     net = counts(products_ref, species) - used
-    back_ref[...] = used.astype(jnp.bfloat16)
-    net_ref[...] = jnp.concatenate([net, net], axis=0).T.astype(jnp.bfloat16)
+    for s in range(species):
+        product = (net[s : s + 1, :] * used).astype(jnp.bfloat16)
+        rows = pl.ds(s * species, species)
+        pairs_ref[rows, : used.shape[1]] = product
+        pairs_ref[rows, used.shape[1] :] = product
     twice = jnp.concatenate([used, used], axis=0).T.astype(jnp.bfloat16)
     constant = jnp.broadcast_to(rate_ref[...], (LANES, rate_ref.shape[1])).T
     pairs = to_species(conc_ref[...].reshape(rows_x * rows_y, width), turn_ref, depth)
@@ -266,35 +290,59 @@
         inverse_ref[:, columns] = 1.0 / conc
         stacked = jnp.concatenate(halves(jnp.log(conc)), axis=0)
         exponent = jnp.dot(twice, stacked, preferred_element_type=jnp.float32)
-        rates_ref[:, columns] = constant * jnp.exp(exponent)
+        rates_ref[:, columns] = jnp.concatenate(halves(constant * jnp.exp(exponent)), axis=0)
+    wide = 2 * LANES
+    copies = []
+    for chunk in range(rates_ref.shape[1] // wide):
+        columns = pl.ds(chunk * wide, wide)
+        block = jnp.dot(pairs_ref[...], rates_ref[:, columns], preferred_element_type=jnp.float32)
+        for part in range(2):
+            jacobian_ref[2 * chunk + part] = block[:, part * LANES : (part + 1) * LANES]
+        tiles = pl.ds(2 * chunk, 2)
+        copies.append(
+            pltpu.make_async_copy(jacobian_ref.at[tiles], jacobian_to.at[tiles], sem.at[chunk])
+        )
+        copies[-1].start()
 
     cond = cond_ref[...]
     rates = cell_rates(cond, diffusivity_ref[...], width, depth)
     to_first, to_last, transfer = factors(rates)
+    forward, backward, gains = sweep_factors(to_first, to_last)
     for k in range(CELLS):
-        first_x_ref[k] = to_first[k]
-        last_x_ref[k] = to_last[k]
+        ends_x_ref[0, k] = to_first[k]
+        ends_x_ref[1, k] = to_last[k]
+        sweep_x_ref[0, k] = forward[k]
+        sweep_x_ref[1, k] = backward[k]
+        sweep_x_ref[2, k] = gains[k] * rates[k]
+        sweep_x_ref[3, k] = to_first[k] * rates[k]
+        sweep_x_ref[4, k] = to_last[k] * rates[k]
     for k in range(4):
         transfer_ref[k] = transfer[k]
     rates = cell_rates(jnp.swapaxes(cond, 0, 1), diffusivity_ref[...], width, depth)
     to_first, to_last, _ = factors(rates)
     lines = jnp.swapaxes(cot_ref[...], 0, 1)
-    local = local_solution([lines[k] for k in range(CELLS)], rates, to_first, to_last)
+    local = local_solution(
+        [lines[k] for k in range(CELLS)], *sweep_factors(to_first, to_last)
+    )
     for k in range(CELLS):
         local_y_ref[k] = local[k] * rates[k]
-        first_y_ref[k] = to_first[k] * rates[k]
-        last_y_ref[k] = to_last[k] * rates[k]
-
-
-def chemistry(field, rates, inverse, net, back):
+        ends_y_ref[0, k] = to_first[k] * rates[k]
+        ends_y_ref[1, k] = to_last[k] * rates[k]
+    for copy in copies:
+        copy.wait()
+
+
+def chemistry(field, columns, jacobian_ref, inverse, vector_ref):
+    species = field.shape[0]
+
     def transposed(vector):
-        stacked = jnp.concatenate(halves(vector), axis=0)
-        flows = jnp.dot(net, stacked, preferred_element_type=jnp.float32) * rates
-        high, low = halves(flows)
-        gathered = jnp.dot(back, high, preferred_element_type=jnp.float32) + jnp.dot(
-            back, low, preferred_element_type=jnp.float32
-        )
-        return gathered * inverse
+        vector_ref[:, columns] = vector
+        sums = [None] * 4
+        for s in range(species):
+            row = jnp.broadcast_to(vector_ref[pl.ds(s, 1), columns], vector.shape)
+            term = row * jacobian_ref[pl.ds(s * species, species), :]
+            sums[s % 4] = term if sums[s % 4] is None else sums[s % 4] + term
+        return ((sums[0] + sums[1]) + (sums[2] + sums[3])) * inverse
 
     third = field + transposed(field) * (1.0 / 3.0)
     second = field + transposed(third) * 0.5
@@ -302,25 +350,32 @@
 
 
 def middle_kernel(
-    depth, ends_ref, local_ref, first_ref, last_ref, rates_ref, inverse_ref, net_ref, back_ref,
-    first_x_ref, last_x_ref, transfer_ref, send_ref, sources_ref, turn_ref,
+    depth, ends_ref, local_ref, ends_y_ref, jacobian_from, inverse_ref, ends_x_ref, transfer_ref,
+    send_ref, sources_ref, turn_ref, vector_ref, jacobian_ref, sem,
 ):
     width = local_ref.shape[2]
+    copies = [
+        pltpu.make_async_copy(jacobian_from.at[tile], jacobian_ref.at[tile], sem.at[tile])
+        for tile in range(jacobian_ref.shape[0])
+    ]
+    for copy in copies:
+        copy.start()
     left, right = get_ends(ends_ref)
     solved = jnp.stack(
-        [local_ref[k] + first_ref[k] * left + last_ref[k] * right for k in range(CELLS)], axis=0
+        [
+            local_ref[k] + ends_y_ref[0, k] * left + ends_y_ref[1, k] * right
+            for k in range(CELLS)
+        ],
+        axis=0,
     )
     solved = jnp.swapaxes(solved, 0, 1).reshape(CELLS * CELLS, width)
-    net = net_ref[...]
-    back = back_ref[...]
     pairs = to_species(solved, turn_ref, depth)
-    columns = pairs[0].shape[1]
     done = []
-    for chunk in range(len(pairs) // 2):
-        at = pl.ds(chunk * 2 * columns, 2 * columns)
-        field = jnp.concatenate(pairs[2 * chunk : 2 * chunk + 2], axis=1)
-        result = chemistry(field, rates_ref[:, at], inverse_ref[:, at], net, back)
-        done += [result[:, :columns], result[:, columns:]]
+    for pair, field in enumerate(pairs):
+        columns = pl.ds(pair * field.shape[1], field.shape[1])
+        copies[pair].wait()
+        jacobian = jacobian_ref.at[pair]
+        done.append(chemistry(field, columns, jacobian, inverse_ref[:, columns], vector_ref))
     changed = from_species(done, turn_ref, depth).reshape(CELLS, CELLS, width)
     sources_ref[...] = changed
     sources = [changed[k] for k in range(CELLS)]
@@ -328,8 +383,8 @@
     put_rows(
         send_ref,
         [
-            total([first_x_ref[k] for k in range(CELLS)], sources),
-            total([last_x_ref[k] for k in range(CELLS)], sources),
+            total([ends_x_ref[0, k] for k in range(CELLS)], sources),
+            total([ends_x_ref[1, k] for k in range(CELLS)], sources),
             *(transfer_ref[k] for k in range(4)),
             blank,
             blank,
@@ -337,17 +392,14 @@
     )
 
 
-def finish_kernel(
-    depth, ends_ref, cond_ref, diffusivity_ref, sources_ref, first_ref, last_ref, out_ref
-):
-    width = out_ref.shape[2]
-    rates = cell_rates(cond_ref[...], diffusivity_ref[...], width, depth)
-    to_first = [first_ref[k] for k in range(CELLS)]
-    to_last = [last_ref[k] for k in range(CELLS)]
-    local = local_solution([sources_ref[k] for k in range(CELLS)], rates, to_first, to_last)
+def finish_kernel(ends_ref, sources_ref, sweep_ref, out_ref):
+    local = local_solution(
+        [sources_ref[k] for k in range(CELLS)],
+        *([sweep_ref[part, k] for k in range(CELLS)] for part in range(3)),
+    )
     left, right = get_ends(ends_ref)
     for k in range(CELLS):
-        out_ref[k] = (local[k] + to_first[k] * left + to_last[k] * right) * rates[k]
+        out_ref[k] = local[k] + sweep_ref[3, k] * left + sweep_ref[4, k] * right
 
 
 def exchange(rows, axis):
@@ -382,24 +434,36 @@
     block = struct(CELLS, CELLS, width)
     send = struct(CELLS * (width // LANES) * ROWS, LANES)
 
-    send_y = call(functools.partial(start_kernel, depth), send)(
-        cotangent, conductance, diffusivity
-    )
-    rates, inverse, net, back, local_y, first_y, last_y, first_x, last_x, transfer = call(
+    send_y = call(
+        functools.partial(start_kernel, depth),
+        send,
+        [
+            pltpu.VMEM(cotangent.shape, jnp.float32),
+            pltpu.VMEM(conductance.shape, jnp.float32),
+            pltpu.VMEM(diffusivity.shape, jnp.float32),
+            pltpu.SemaphoreType.DMA((3,)),
+        ],
+        far_in=(0, 1, 2),
+    )(cotangent, conductance, diffusivity)
+    jacobian, inverse, local_y, ends_y, ends_x, sweep_x, transfer = call(
         functools.partial(prepare_kernel, depth),
         [
-            struct(reactions, columns),
+            struct(columns // LANES, species * species, LANES),
             struct(species, columns),
-            jax.ShapeDtypeStruct((reactions, 2 * species), jnp.bfloat16),
-            jax.ShapeDtypeStruct((species, reactions), jnp.bfloat16),
             block,
-            block,
-            block,
-            block,
-            block,
+            struct(2, CELLS, CELLS, width),
+            struct(2, CELLS, CELLS, width),
+            struct(5, CELLS, CELLS, width),
             struct(4, CELLS, width),
         ],
-        [turn],
+        [
+            turn,
+            pltpu.VMEM((2 * reactions, columns), jnp.bfloat16),
+            pltpu.VMEM((species * species, 2 * reactions), jnp.bfloat16),
+            pltpu.VMEM((columns // LANES, species * species, LANES), jnp.float32),
+            pltpu.SemaphoreType.DMA((columns // (2 * LANES),)),
+        ],
+        far_out=(0,),
     )(
         cotangent,
         concentration,
@@ -409,14 +473,20 @@
         reactants.T,
         products.T,
     )
-    ends_y = solve_lines(send_y, "gy")
-    send_x, sources = call(functools.partial(middle_kernel, depth), [send, block], [turn])(
-        ends_y, local_y, first_y, last_y, rates, inverse, net, back, first_x, last_x, transfer
-    )
-    ends_x = solve_lines(send_x, "gx")
-    return call(functools.partial(finish_kernel, depth), block)(
-        ends_x, conductance, diffusivity, sources, first_x, last_x
-    )
+    got_y = solve_lines(send_y, "gy")
+    send_x, sources = call(
+        functools.partial(middle_kernel, depth),
+        [send, block],
+        [
+            turn,
+            pltpu.VMEM((species, columns), jnp.float32),
+            pltpu.VMEM((columns // LANES, species * species, LANES), jnp.float32),
+            pltpu.SemaphoreType.DMA((columns // LANES,)),
+        ],
+        far_in=(3,),
+    )(got_y, local_y, ends_y, jacobian, inverse, ends_x, transfer)
+    got_x = solve_lines(send_x, "gx")
+    return call(finish_kernel, block)(got_x, sources, sweep_x)
 
 
 def solution(mesh):

time: 72 us -> 73.4 us (1.019)
  waiting for transfers between devices: 6.04 us -> 0.01 us
  local copies, waits for them, and re-layouts: 2.99 us -> 7.2 us
  Pallas kernels: 6.91 us -> 9.94 us
    all_to_all x1, waiting for transfers between devices: 6.04 us -> 0.01 us  [exchange(): return lax.all_to_all(blocks, axis, 0, 0, tiled=True).reshape(rows.shape)]
    unnamed x18 -> x16, local copies, waits for them, and re-layouts: 2.99 us -> 7.2 us
    pallas_call x6, Pallas kernels: 6.91 us -> 9.94 us  [run(): pl.pallas_call(kernel, out_shape=out_shape, in_specs=[far if k in far_in...]
  transfers between devices with their start and end apart: 1 -> 1, of which waited for: 1 -> 0; matrix products, arithmetic and copies ran while one was open for 0% -> 0% of each run, Pallas kernels for 1% -> 6%
where the time goes in v3:
time: 73.4 us; the launch traced here: 72.9 us
  blocking collectives  52.2 us (71%)
  Pallas kernels  9.94 us (14%)
  local copies, waits for them, and re-layouts  7.2 us (10%)
  starting transfers between devices  3.5 us (5%)
    all_to_all x3, blocking collectives, exchange(): return lax.all_to_all(blocks, axis, 0, 0, tiled=True).reshape(rows.shape)  52.2 us
    pallas_call x6, Pallas kernels, run(): pl.pallas_call(kernel, out_shape=out_shape, in_specs=[far if k in far_in...  9.94 us
    unnamed x16, local copies, waits for them, and re-layouts  7.2 us
    all_to_all x1, starting transfers between devices, exchange(): return lax.all_to_all(blocks, axis, 0, 0, tiled=True).reshape(rows.shape)  3.5 us
  transfers between devices with their start and end apart: 1, of which 0 were waited for; matrix products, arithmetic and copies ran while one was open for 0% of the time, Pallas kernels for 6%

profile of v3, /device:TPU:8, one launch (start us, length us, event | category | flops | bytes accessed | tf_op | source)
XLA Modules:
  0.0 72.9 jit_solution(4286144498932737048)
XLA Ops:
  0.0 1.4 %shard_map.73 = f32[256,128]{1,0:T(8,128)S(1)} custom-call(f32[8,8,512]{2,1,0:T(8,128)} %cot_ref.1, f32[8,8,16]{2,1,0:T(8,128)} %cond_ref.1, f32[1,32]{1,0:T(1,128)} %bitcast.21), custom_call_target="tpu_custom_call" | custom-call | tf_op jit(solution)/shard_map/pallas_call | solution.py:29
  1.4 18.9 %all_to_all.20 = f32[16,16,128]{2,1,0:T(8,128)S(1)} all-to-all(f32[16,16,128]{2,1,0:T(8,128)S(1)} %bitcast.14), channel_id=1, replica_groups=mesh['gx'=32,'gy'=16] {'gy'}, dimensions={0} | all-to-all | bytes 262144 | tf_op jit(solution)/shard_map/all_to_all | solution.py:408
  20.3 0.8 %shard_map.74 = f32[64,128]{1,0:T(8,128)} custom-call(f32[256,128]{1,0:T(8,128)S(1)} %bitcast.12), custom_call_target="tpu_custom_call" | custom-call | tf_op jit(solution)/shard_map/pallas_call | solution.py:29
  21.0 3.5 %all-to-all-start.1 = ((f32[16,4,128]{2,1,0:T(4,128)}), f32[16,4,128]{2,1,0:T(4,128)S(1)}, u32[]{:S(2)}, u32[]{:S(2)}) async-start(f32[16,4,128]{2,1,0:T(4,128)} %bitcast.3), calls=%async_computation.1 | async-start | bytes 65536 | tf_op jit(solution)/shard_map/all_to_all | solution.py:408
  24.5 0.0 copy-start.1
  24.5 0.9 %copy-done.1 = f32[8,8,512]{2,1,0:T(8,128)S(1)} copy-done((f32[8,8,512]{2,1,0:T(8,128)S(1)}, f32[8,8,512]{2,1,0:T(8,128)}, u32[]{:S(2)}) %copy-start.1) | copy-done | bytes 131096
  25.4 0.0 copy-start.2
  25.4 0.8 %copy-done.2 = f32[8,8,16]{2,1,0:T(8,128)S(1)} copy-done((f32[8,8,16]{2,1,0:T(8,128)S(1)}, f32[8,8,16]{2,1,0:T(8,128)}, u32[]{:S(2)}) %copy-start.2) | copy-done | bytes 4120
  26.2 0.0 copy-start.3
  26.2 0.9 %copy-done.3 = f32[8,8,512]{2,1,0:T(8,128)S(1)} copy-done((f32[8,8,512]{2,1,0:T(8,128)S(1)}, f32[8,8,512]{2,1,0:T(8,128)}, u32[]{:S(2)}) %copy-start.3) | copy-done | bytes 131096
  27.1 0.0 copy-start.4
  27.1 0.7 copy-done.4
  27.8 0.0 copy-start.5
  27.8 0.7 copy-done.5
  28.5 0.0 copy-start.6
  28.5 0.7 copy-done.6
  29.1 0.0 copy-start.7
  29.1 0.7 copy-done.7
  29.8 4.2 %shard_map.75 = (f32[8,1024,128]{2,1,0:T(8,128)S(1)}, f32[32,1024]{1,0:T(8,128)S(1)}, f32[8,8,512]{2,1,0:T(8,128)S(1)}, f32[2,8,8,512]{3,2,1,0:T(8,128)S(1)}, f3...) custom-call(f32[8,8,512]{2,1,0:T(8,128)S(1)} %copy-done.1, ...), custom_call_target="tpu_custom_call" | custom-call | tf_op jit(solution)/shard_map/pallas_call | solution.py:29
  34.0 0.0 copy-start
  34.0 1.9 %copy-done = f32[8,1024,128]{2,1,0:T(8,128)} copy-done((f32[8,1024,128]{2,1,0:T(8,128)}, f32[8,1024,128]{2,1,0:T(8,128)S(1)}, u32[]{:S(2)}) %copy-start) | copy-done | bytes 4194328
  36.0 0.0 all-to-all-done.1
  36.0 2.7 %shard_map.76 = (f32[256,128]{1,0:T(8,128)S(1)}, f32[8,8,512]{2,1,0:T(8,128)S(1)}) custom-call(f32[64,128]{1,0:T(8,128)S(1)} %bitcast.15, f32[8,8,512]{2,1,0:T(8,128)S(1)} %get-tuple-element.14.local_ref, f32[2,8,8,512]{3,2,1,0:T(8,128)S(1)} %get-tuple-element.15.ends_y_ref, f32[8,1024,128]{2,1,0:T(8,128)} %copy-done, ...), custom_call_target="tpu_custom_call" | custom-call | tf_op jit(solution)/shard_map/pallas_call | solution.py:29
  38.7 20.4 %all_to_all.21 = f32[32,8,128]{2,1,0:T(8,128)S(1)} all-to-all(f32[32,8,128]{2,1,0:T(8,128)S(1)} %bitcast.17), channel_id=1, replica_groups=mesh['gx'=32,'gy'=16] {'gx'}, dimensions={0} | all-to-all | bytes 262144 | tf_op jit(solution)/shard_map/all_to_all | solution.py:408
  59.1 0.2 shard_map.77
  59.3 12.9 %all_to_all.22 = f32[32,2,128]{2,1,0:T(2,128)S(1)} all-to-all(f32[32,2,128]{2,1,0:T(2,128)S(1)} %bitcast.16), channel_id=1, replica_groups=mesh['gx'=32,'gy'=16] {'gx'}, dimensions={0} | all-to-all | bytes 65536 | tf_op jit(solution)/shard_map/all_to_all | solution.py:408
  72.2 0.7 shard_map.78
Async XLA Ops:
  21.0 15.0 %all-to-all-start.1 = ((f32[16,4,128]{2,1,0:T(4,128)}), f32[16,4,128]{2,1,0:T(4,128)S(1)}, u32[]{:S(2)}, u32[]{:S(2)}) async-start(f32[16,4,128]{2,1,0:T(4,128)} %bitcast.3), calls=%async_computation.1 | async-start | bytes 65536 | tf_op jit(solution)/shard_map/all_to_all | solution.py:408
  24.5 0.9 %copy-start.1 = (f32[8,8,512]{2,1,0:T(8,128)S(1)}, f32[8,8,512]{2,1,0:T(8,128)}, u32[]{:S(2)}) copy-start(f32[8,8,512]{2,1,0:T(8,128)} %cot_ref.1) | copy-start | bytes 393220
  25.4 0.8 %copy-start.2 = (f32[8,8,16]{2,1,0:T(8,128)S(1)}, f32[8,8,16]{2,1,0:T(8,128)}, u32[]{:S(2)}) copy-start(f32[8,8,16]{2,1,0:T(8,128)} %cond_ref.1) | copy-start | bytes 12292
  26.2 0.9 %copy-start.3 = (f32[8,8,512]{2,1,0:T(8,128)S(1)}, f32[8,8,512]{2,1,0:T(8,128)}, u32[]{:S(2)}) copy-start(f32[8,8,512]{2,1,0:T(8,128)} %conc_ref.1) | copy-start | bytes 393220
  27.1 0.7 copy-start.4
  27.8 0.7 copy-start.5
  28.5 0.7 copy-start.6
  29.1 0.7 copy-start.7
  34.0 2.0 %copy-start = (f32[8,1024,128]{2,1,0:T(8,128)}, f32[8,1024,128]{2,1,0:T(8,128)S(1)}, u32[]{:S(2)}) copy-start(f32[8,1024,128]{2,1,0:T(8,128)S(1)} %get-tuple-element.16.jacobian_from) | copy-start | bytes 12582916

commit v4 on v3

--- a/solution.py
+++ b/solution.py
@@ -42,6 +42,13 @@
     return jax.ShapeDtypeStruct(shape, jnp.float32)
 
 
+def begin(pairs, sem):
+    copies = [pltpu.make_async_copy(*pair, sem.at[k]) for k, pair in enumerate(pairs)]
+    for copy in copies:
+        copy.start()
+    return copies
+
+
 def cell_rates(cond, diffusivity, width, depth):
     lane = lax.broadcasted_iota(jnp.int32, (depth, width), 1)
     same_depth = lax.rem(lane, depth) == lax.broadcasted_iota(jnp.int32, (depth, width), 0)
@@ -137,20 +144,17 @@
     depth, cot_from, cond_from, diffusivity_from, send_ref, cot_ref, cond_ref, diffusivity_ref, sem
 ):
     width = cot_ref.shape[2]
-    copies = [
-        pltpu.make_async_copy(cond_from, cond_ref, sem.at[0]),
-        pltpu.make_async_copy(diffusivity_from, diffusivity_ref, sem.at[1]),
-        pltpu.make_async_copy(cot_from, cot_ref, sem.at[2]),
-    ]
-    for copy in copies:
-        copy.start()
-    for copy in copies:
-        copy.wait()
-    lines = jnp.swapaxes(cot_ref[...], 0, 1)
+    copies = begin(
+        [(cond_from, cond_ref), (diffusivity_from, diffusivity_ref), (cot_from, cot_ref)], sem
+    )
+    copies[0].wait()
+    copies[1].wait()
     cond = jnp.swapaxes(cond_ref[...], 0, 1)
-    sources = [lines[cell] for cell in range(CELLS)]
     rates = cell_rates(cond, diffusivity_ref[...], width, depth)
     to_first, to_last, transfer = factors(rates)
+    copies[2].wait()
+    lines = jnp.swapaxes(cot_ref[...], 0, 1)
+    sources = [lines[cell] for cell in range(CELLS)]
     blank = jnp.zeros_like(rates[0])
     put_rows(
         send_ref,
@@ -269,10 +273,25 @@
 
 
 def prepare_kernel(
-    depth, cot_ref, conc_ref, cond_ref, diffusivity_ref, rate_ref, reactants_ref, products_ref,
-    jacobian_to, inverse_ref, local_y_ref, ends_y_ref, ends_x_ref, sweep_x_ref, transfer_ref,
-    turn_ref, rates_ref, pairs_ref, jacobian_ref, sem,
+    depth, cot_from, conc_from, cond_from, diffusivity_from, rate_from, reactants_from,
+    products_from, jacobian_to, inverse_ref, local_y_ref, ends_y_ref, ends_x_ref, sweep_x_ref,
+    transfer_ref, cot_ref, conc_ref, cond_ref, diffusivity_ref, rate_ref, reactants_ref,
+    products_ref, turn_ref, rates_ref, pairs_ref, jacobian_ref, in_sem, sem,
 ):
+    inputs = begin(
+        [
+            (reactants_from, reactants_ref),
+            (products_from, products_ref),
+            (rate_from, rate_ref),
+            (conc_from, conc_ref),
+            (cond_from, cond_ref),
+            (diffusivity_from, diffusivity_ref),
+            (cot_from, cot_ref),
+        ],
+        in_sem,
+    )
+    for copy in inputs:
+        copy.wait()
     rows_x, rows_y, width = conc_ref.shape
     species = width // depth
     used = counts(reactants_ref, species)
@@ -354,12 +373,8 @@
     send_ref, sources_ref, turn_ref, vector_ref, jacobian_ref, sem,
 ):
     width = local_ref.shape[2]
-    copies = [
-        pltpu.make_async_copy(jacobian_from.at[tile], jacobian_ref.at[tile], sem.at[tile])
-        for tile in range(jacobian_ref.shape[0])
-    ]
-    for copy in copies:
-        copy.start()
+    tiles = range(jacobian_ref.shape[0])
+    copies = begin([(jacobian_from.at[tile], jacobian_ref.at[tile]) for tile in tiles], sem)
     left, right = get_ends(ends_ref)
     solved = jnp.stack(
         [
@@ -448,7 +463,7 @@
     jacobian, inverse, local_y, ends_y, ends_x, sweep_x, transfer = call(
         functools.partial(prepare_kernel, depth),
         [
-            struct(columns // LANES, species * species, LANES),
+            pltpu.HBM((columns // LANES, species * species, LANES), jnp.float32),
             struct(species, columns),
             block,
             struct(2, CELLS, CELLS, width),
@@ -457,12 +472,21 @@
             struct(4, CELLS, width),
         ],
         [
+            pltpu.VMEM(cotangent.shape, jnp.float32),
+            pltpu.VMEM(concentration.shape, jnp.float32),
+            pltpu.VMEM(conductance.shape, jnp.float32),
+            pltpu.VMEM(diffusivity.shape, jnp.float32),
+            pltpu.VMEM((1, reactions), jnp.float32),
+            pltpu.VMEM((2, reactions), jnp.int32),
+            pltpu.VMEM((2, reactions), jnp.int32),
             turn,
             pltpu.VMEM((2 * reactions, columns), jnp.bfloat16),
             pltpu.VMEM((species * species, 2 * reactions), jnp.bfloat16),
             pltpu.VMEM((columns // LANES, species * species, LANES), jnp.float32),
+            pltpu.SemaphoreType.DMA((7,)),
             pltpu.SemaphoreType.DMA((columns // (2 * LANES),)),
         ],
+        far_in=tuple(range(7)),
         far_out=(0,),
     )(
         cotangent,

time: 73.4 us -> 68.9 us (0.939)
  local copies, waits for them, and re-layouts: 7.2 us -> 0 us
  waiting for transfers between devices: 0.01 us -> 3.31 us
    unnamed x16 -> x0, local copies, waits for them, and re-layouts: 7.2 us -> none
    all_to_all x1, waiting for transfers between devices: 0.01 us -> 3.31 us  [exchange(): return lax.all_to_all(blocks, axis, 0, 0, tiled=True).reshape(rows.shape)]
  transfers between devices with their start and end apart: 1 -> 1, of which waited for: 0 -> 1; matrix products, arithmetic and copies ran while one was open for 0% -> 0% of each run, Pallas kernels for 6% -> 6%
where the time goes in v4:
time: 68.9 us; the launch traced here: 68.6 us
  blocking collectives  51.8 us (75%)
  Pallas kernels  9.92 us (14%)
  starting transfers between devices  3.5 us (5%)
  waiting for transfers between devices  3.31 us (5%)
    all_to_all x3, blocking collectives, exchange(): return lax.all_to_all(blocks, axis, 0, 0, tiled=True).reshape(rows.shape)  51.8 us
    pallas_call x6, Pallas kernels, run(): pl.pallas_call(kernel, out_shape=out_shape, in_specs=[far if k in far_in...  9.92 us
    all_to_all x1, starting transfers between devices, exchange(): return lax.all_to_all(blocks, axis, 0, 0, tiled=True).reshape(rows.shape)  3.5 us
    all_to_all x1, waiting for transfers between devices, exchange(): return lax.all_to_all(blocks, axis, 0, 0, tiled=True).reshape(rows.shape)  3.31 us
  transfers between devices with their start and end apart: 1, of which 1 were waited for; matrix products, arithmetic and copies ran while one was open for 0% of the time, Pallas kernels for 6%

profile of v4, /device:TPU:8, one launch (start us, length us, event | category | flops | bytes accessed | tf_op | source)
XLA Modules:
  0.0 68.6 jit_solution(14005313117569386)
XLA Ops:
  0.0 1.2 %shard_map.73 = f32[256,128]{1,0:T(8,128)S(1)} custom-call(f32[8,8,512]{2,1,0:T(8,128)} %cot_from.3, f32[8,8,16]{2,1,0:T(8,128)} %cond_from.3, f32[1,32]{1,0:T(1,128)} %bitcast.21), custom_call_target="tpu_custom_call" | custom-call | tf_op jit(solution)/shard_map/pallas_call | solution.py:29
  1.3 18.9 %all_to_all.20 = f32[16,16,128]{2,1,0:T(8,128)S(1)} all-to-all(f32[16,16,128]{2,1,0:T(8,128)S(1)} %bitcast.14), channel_id=1, replica_groups=mesh['gx'=32,'gy'=16] {'gy'}, dimensions={0} | all-to-all | bytes 262144 | tf_op jit(solution)/shard_map/all_to_all | solution.py:423
  20.1 0.8 %shard_map.74 = f32[64,128]{1,0:T(8,128)} custom-call(f32[256,128]{1,0:T(8,128)S(1)} %bitcast.12), custom_call_target="tpu_custom_call" | custom-call | tf_op jit(solution)/shard_map/pallas_call | solution.py:29
  20.9 3.5 %all-to-all-start.1 = ((f32[16,4,128]{2,1,0:T(4,128)}), f32[16,4,128]{2,1,0:T(4,128)S(1)}, u32[]{:S(2)}, u32[]{:S(2)}) async-start(f32[16,4,128]{2,1,0:T(4,128)} %bitcast.3), calls=%async_computation.1 | async-start | bytes 65536 | tf_op jit(solution)/shard_map/all_to_all | solution.py:423
  24.4 4.3 %shard_map.75 = (f32[8,1024,128]{2,1,0:T(8,128)}, f32[32,1024]{1,0:T(8,128)S(1)}, f32[8,8,512]{2,1,0:T(8,128)S(1)}, f32[2,8,8,512]{3,2,1,0:T(8,128)S(1)}, f32[2,...) custom-call(f32[8,8,512]{2,1,0:T(8,128)} %cot_from.3, f32[8,8,512]{2,1,0:T(8,128)} %conc_from.1, ...), custom_call_target="tpu_custom_call" | custom-call | tf_op jit(solution)/shard_map/pallas_call | solution.py:29
  28.7 3.3 %all-to-all-done.1 = f32[16,4,128]{2,1,0:T(4,128)S(1)} async-done(((f32[16,4,128]{2,1,0:T(4,128)}), f32[16,4,128]{2,1,0:T(4,128)S(1)}, u32[]{:S(2)}, u32[]{:S(2)}) %all-to-all-start.1) | async-done | bytes 32800 | tf_op jit(solution)/shard_map/all_to_all | solution.py:423
  32.0 2.7 %shard_map.76 = (f32[256,128]{1,0:T(8,128)S(1)}, f32[8,8,512]{2,1,0:T(8,128)S(1)}) custom-call(f32[64,128]{1,0:T(8,128)S(1)} %bitcast.15, f32[8,8,512]{2,1,0:T(8,128)S(1)} %get-tuple-element.14.local_ref, f32[2,8,8,512]{3,2,1,0:T(8,128)S(1)} %get-tuple-element.15.ends_y_ref, f32[8,1024,128]{2,1,0:T(8,128)} %get-tuple-element.16.jacobian_from, ...), custom_call_target="tpu_custom_call" | custom-call | tf_op jit(solution)/shard_map/pallas_call | solution.py:29
  34.8 19.9 %all_to_all.21 = f32[32,8,128]{2,1,0:T(8,128)S(1)} all-to-all(f32[32,8,128]{2,1,0:T(8,128)S(1)} %bitcast.17), channel_id=1, replica_groups=mesh['gx'=32,'gy'=16] {'gx'}, dimensions={0} | all-to-all | bytes 262144 | tf_op jit(solution)/shard_map/all_to_all | solution.py:423
  54.7 0.2 shard_map.77
  54.9 13.0 %all_to_all.22 = f32[32,2,128]{2,1,0:T(2,128)S(1)} all-to-all(f32[32,2,128]{2,1,0:T(2,128)S(1)} %bitcast.16), channel_id=1, replica_groups=mesh['gx'=32,'gy'=16] {'gx'}, dimensions={0} | all-to-all | bytes 65536 | tf_op jit(solution)/shard_map/all_to_all | solution.py:423
  67.8 0.7 %shard_map.78 = f32[8,8,512]{2,1,0:T(8,128)} custom-call(f32[64,128]{1,0:T(8,128)S(1)} %bitcast.18, f32[8,8,512]{2,1,0:T(8,128)S(1)} %get-tuple-element.21.sources_ref, f32[5,8,8,512]{3,2,1,0:T(8,128)S(1)} %get-tuple-element.22.sweep_ref), custom_call_target="tpu_custom_call" | custom-call | tf_op jit(solution)/shard_map/pallas_call | solution.py:29
Async XLA Ops:
  20.9 11.2 %all-to-all-start.1 = ((f32[16,4,128]{2,1,0:T(4,128)}), f32[16,4,128]{2,1,0:T(4,128)S(1)}, u32[]{:S(2)}, u32[]{:S(2)}) async-start(f32[16,4,128]{2,1,0:T(4,128)} %bitcast.3), calls=%async_computation.1 | async-start | bytes 65536 | tf_op jit(solution)/shard_map/all_to_all | solution.py:423

commit v5 on v4

--- a/solution.py
+++ b/solution.py
@@ -10,7 +10,8 @@
 
 CELLS = 8
 LANES = 128
-ROWS = 8
+ROWS = 4
+NEAR = 3
 LIMIT = 16 << 20
 
 
@@ -49,49 +50,47 @@
     return copies
 
 
-def cell_rates(cond, diffusivity, width, depth):
-    lane = lax.broadcasted_iota(jnp.int32, (depth, width), 1)
-    same_depth = lax.rem(lane, depth) == lax.broadcasted_iota(jnp.int32, (depth, width), 0)
+def species_scale(diffusivity, width, depth):
     species = width // depth
     lane = lax.broadcasted_iota(jnp.int32, (species, width), 1)
-    same_species = lax.div(lane, depth) == lax.broadcasted_iota(jnp.int32, (species, width), 0)
-    highest = lax.Precision.HIGHEST
+    same = lax.div(lane, depth) == lax.broadcasted_iota(jnp.int32, (species, width), 0)
+    return jnp.dot(
+        jnp.broadcast_to(1.0 / diffusivity, (CELLS, species)),
+        same.astype(jnp.float32),
+        precision=lax.Precision.HIGHEST,
+        preferred_element_type=jnp.float32,
+    )
+
+
+def cell_rates(cond, scale, depth):
+    width = scale.shape[1]
+    lane = lax.broadcasted_iota(jnp.int32, (depth, width), 1)
+    same = lax.rem(lane, depth) == lax.broadcasted_iota(jnp.int32, (depth, width), 0)
     spread = jnp.dot(
         (1.0 / cond).reshape(-1, depth),
-        same_depth.astype(jnp.float32),
-        precision=highest,
-        preferred_element_type=jnp.float32,
-    )
-    scale = jnp.dot(
-        jnp.broadcast_to(1.0 / diffusivity, (CELLS, species)),
-        same_species.astype(jnp.float32),
-        precision=highest,
+        same.astype(jnp.float32),
+        precision=lax.Precision.HIGHEST,
         preferred_element_type=jnp.float32,
     )
     tiles = spread.reshape(CELLS, CELLS, width)
     return [tiles[cell] * scale for cell in range(CELLS)]
 
 
+def shoot(rates, value, step, order):
+    values = [None] * CELLS
+    for cell in order:
+        values[cell] = value
+        step = step + rates[cell] * value
+        value = value + step
+    return values, value, step
+
+
 def factors(rates):
     one = jnp.ones_like(rates[0])
-    zero = jnp.zeros_like(one)
-
-    def shoot(value, step, order):
-        values = {}
-        for cell in order:
-            values[cell] = value
-            step = step + rates[cell] * value
-            value = value + step
-        return values, value, step
-
-    flat, flat_out, flat_step = shoot(one, zero, range(CELLS))
-    slope, slope_out, slope_step = shoot(zero, one, range(CELLS))
-    right, _, _ = shoot(one, one, reversed(range(CELLS)))
-    inverse = 1.0 / (flat_out + slope_out)
-    to_last = [(flat[k] + slope[k]) * inverse for k in range(CELLS)]
-    to_first = [right[k] * inverse for k in range(CELLS)]
-    transfer = (flat_step, slope_step, flat[CELLS - 1], slope[CELLS - 1])
-    return to_first, to_last, transfer
+    left, out, _ = shoot(rates, one, one, range(CELLS))
+    right, _, _ = shoot(rates, one, one, reversed(range(CELLS)))
+    inverse = 1.0 / out
+    return [value * inverse for value in right], [value * inverse for value in left]
 
 
 def sweep_factors(to_first, to_last):
@@ -125,10 +124,15 @@
 
 def put_rows(send_ref, rows):
     for row, value in enumerate(rows):
-        for tile in range(value.shape[1] // LANES):
-            send_ref[pl.ds(tile * ROWS + row, CELLS, stride=CELLS * 4), :] = value[
-                :, tile * LANES : (tile + 1) * LANES
-            ]
+        for tile in range(4):
+            part = value
+            if value.shape[1] > LANES:
+                part = value[:, tile * LANES : (tile + 1) * LANES]
+            send_ref[pl.ds(tile * ROWS + row, CELLS, stride=4 * ROWS), :] = part
+
+
+def pack(cond):
+    return jnp.concatenate([cond[cell] for cell in range(CELLS)], axis=1)
 
 
 def get_ends(back_ref):
@@ -141,7 +145,8 @@
 
 
 def start_kernel(
-    depth, cot_from, cond_from, diffusivity_from, send_ref, cot_ref, cond_ref, diffusivity_ref, sem
+    depth, cot_from, cond_from, diffusivity_from, send_ref, scale_ref, cot_ref, cond_ref,
+    diffusivity_ref, sem,
 ):
     width = cot_ref.shape[2]
     copies = begin(
@@ -150,28 +155,46 @@
     copies[0].wait()
     copies[1].wait()
     cond = jnp.swapaxes(cond_ref[...], 0, 1)
-    rates = cell_rates(cond, diffusivity_ref[...], width, depth)
-    to_first, to_last, transfer = factors(rates)
+    scale = species_scale(diffusivity_ref[...], width, depth)
+    to_first, to_last = factors(cell_rates(cond, scale, depth))
+    packed = pack(cond)
+    for tile in range(4):
+        scale_ref[pl.ds(tile, 1), :] = scale[0:1, tile * LANES : (tile + 1) * LANES]
     copies[2].wait()
     lines = jnp.swapaxes(cot_ref[...], 0, 1)
     sources = [lines[cell] for cell in range(CELLS)]
-    blank = jnp.zeros_like(rates[0])
     put_rows(
         send_ref,
-        [total(to_first, sources), total(to_last, sources), *transfer, blank, blank],
-    )
-
-
-def solve_kernel(blocks, tiles, got_ref, out_ref, *scratch):
-    value_l, step_l, value_r, step_r, ratio_l, add_l, ratio_r, add_r, sum_l, sum_r = scratch
+        [total(to_first, sources), total(to_last, sources), packed, jnp.zeros_like(packed)],
+    )
+
+
+def solve_kernel(depth, axis, blocks, tiles, got_ref, scale_ref, out_ref, *scratch):
+    value_l, step_l, value_r, step_r, ratio_l, add_l, ratio_r, add_r, sum_l, sum_r = scratch[:10]
+    moves = scratch[10:]
+    me = lax.axis_index(axis)
     one = jnp.ones((1, LANES), jnp.float32)
-
-    def pick(block, tile, row):
-        return got_ref[pl.ds((block * tiles + tile) * ROWS + row, 1), :]
 
     def whole(tile, row):
         return got_ref[pl.ds(tile * ROWS + row, blocks, stride=ROWS * tiles), :]
 
+    for tile in range(tiles):
+        scale = scale_ref[pl.ds(lax.rem(me * tiles + tile, 4), 1), :]
+        inverse = 1.0 / whole(tile, 2)
+        lane = lax.rem(lax.broadcasted_iota(jnp.int32, inverse.shape, 1), depth)
+        rates = [
+            jnp.take_along_axis(
+                inverse, lane + cell * depth, axis=1, mode="promise_in_bounds"
+            )
+            * scale
+            for cell in range(CELLS)
+        ]
+        ones = jnp.ones_like(inverse)
+        flat, _, flat_step = shoot(rates, ones, ones * 0.0, range(CELLS))
+        slope, _, slope_step = shoot(rates, ones * 0.0, ones, range(CELLS))
+        last = CELLS - 1
+        for move, value in zip(moves, (flat_step, slope_step, flat[last], slope[last]), strict=True):
+            move[tile] = value
     for tile in range(tiles):
         left, left_step, right, right_step = one, one, one, one
         for block in range(blocks):
@@ -180,11 +203,11 @@
             step_l[tile, pl.ds(block, 1), :] = left_step
             value_r[tile, pl.ds(mirror + 1, 1), :] = right
             step_r[tile, pl.ds(mirror + 1, 1), :] = right_step
-            c, d, e, f = (pick(block, tile, row) for row in range(2, 6))
+            c, d, e, f = (move[tile, pl.ds(block, 1), :] for move in moves)
             kept = e * left + f * left_step
             left_step = c * left + d * left_step
             left = kept + left_step
-            c, d, e, f = (pick(mirror, tile, row) for row in range(2, 6))
+            c, d, e, f = (move[tile, pl.ds(mirror, 1), :] for move in moves)
             kept = d * right + f * right_step
             right_step = c * right + e * right_step
             right = kept + right_step
@@ -274,8 +297,8 @@
 
 def prepare_kernel(
     depth, cot_from, conc_from, cond_from, diffusivity_from, rate_from, reactants_from,
-    products_from, jacobian_to, inverse_ref, local_y_ref, ends_y_ref, ends_x_ref, sweep_x_ref,
-    transfer_ref, cot_ref, conc_ref, cond_ref, diffusivity_ref, rate_ref, reactants_ref,
+    products_from, jacobian_to, jacobian_near_ref, inverse_ref, local_y_ref, ends_y_ref,
+    ends_x_ref, sweep_x_ref, packed_x_ref, cot_ref, conc_ref, cond_ref, diffusivity_ref, rate_ref, reactants_ref,
     products_ref, turn_ref, rates_ref, pairs_ref, jacobian_ref, in_sem, sem,
 ):
     inputs = begin(
@@ -316,16 +339,23 @@
         columns = pl.ds(chunk * wide, wide)
         block = jnp.dot(pairs_ref[...], rates_ref[:, columns], preferred_element_type=jnp.float32)
         for part in range(2):
-            jacobian_ref[2 * chunk + part] = block[:, part * LANES : (part + 1) * LANES]
-        tiles = pl.ds(2 * chunk, 2)
-        copies.append(
-            pltpu.make_async_copy(jacobian_ref.at[tiles], jacobian_to.at[tiles], sem.at[chunk])
-        )
-        copies[-1].start()
+            tile = 2 * chunk + part - jacobian_ref.shape[0]
+            value = block[:, part * LANES : (part + 1) * LANES]
+            if tile >= 0:
+                jacobian_near_ref[tile] = value
+                continue
+            tile += jacobian_ref.shape[0]
+            jacobian_ref[tile] = value
+            copies.append(
+                pltpu.make_async_copy(jacobian_ref.at[tile], jacobian_to.at[tile], sem.at[tile])
+            )
+            copies[-1].start()
 
     cond = cond_ref[...]
-    rates = cell_rates(cond, diffusivity_ref[...], width, depth)
-    to_first, to_last, transfer = factors(rates)
+    scale = species_scale(diffusivity_ref[...], width, depth)
+    packed_x_ref[...] = pack(cond)
+    rates = cell_rates(cond, scale, depth)
+    to_first, to_last = factors(rates)
     forward, backward, gains = sweep_factors(to_first, to_last)
     for k in range(CELLS):
         ends_x_ref[0, k] = to_first[k]
@@ -335,14 +365,10 @@
         sweep_x_ref[2, k] = gains[k] * rates[k]
         sweep_x_ref[3, k] = to_first[k] * rates[k]
         sweep_x_ref[4, k] = to_last[k] * rates[k]
-    for k in range(4):
-        transfer_ref[k] = transfer[k]
-    rates = cell_rates(jnp.swapaxes(cond, 0, 1), diffusivity_ref[...], width, depth)
-    to_first, to_last, _ = factors(rates)
+    rates = cell_rates(jnp.swapaxes(cond, 0, 1), scale, depth)
+    to_first, to_last = factors(rates)
     lines = jnp.swapaxes(cot_ref[...], 0, 1)
-    local = local_solution(
-        [lines[k] for k in range(CELLS)], *sweep_factors(to_first, to_last)
-    )
+    local = local_solution([lines[k] for k in range(CELLS)], *sweep_factors(to_first, to_last))
     for k in range(CELLS):
         local_y_ref[k] = local[k] * rates[k]
         ends_y_ref[0, k] = to_first[k] * rates[k]
@@ -369,12 +395,14 @@
 
 
 def middle_kernel(
-    depth, ends_ref, local_ref, ends_y_ref, jacobian_from, inverse_ref, ends_x_ref, transfer_ref,
-    send_ref, sources_ref, turn_ref, vector_ref, jacobian_ref, sem,
+    depth, ends_ref, local_ref, ends_y_ref, jacobian_from, jacobian_near_ref, inverse_ref,
+    ends_x_ref, packed_x_ref, send_ref, sources_ref, turn_ref, vector_ref, jacobian_ref, sem,
 ):
     width = local_ref.shape[2]
-    tiles = range(jacobian_ref.shape[0])
-    copies = begin([(jacobian_from.at[tile], jacobian_ref.at[tile]) for tile in tiles], sem)
+    far = jacobian_ref.shape[0]
+    copies = begin(
+        [(jacobian_from.at[tile], jacobian_ref.at[tile]) for tile in range(far)], sem
+    )
     left, right = get_ends(ends_ref)
     solved = jnp.stack(
         [
@@ -385,24 +413,27 @@
     )
     solved = jnp.swapaxes(solved, 0, 1).reshape(CELLS * CELLS, width)
     pairs = to_species(solved, turn_ref, depth)
-    done = []
-    for pair, field in enumerate(pairs):
+    done = [None] * len(pairs)
+    for pair in [*range(far, len(pairs)), *range(far)]:
+        field = pairs[pair]
         columns = pl.ds(pair * field.shape[1], field.shape[1])
-        copies[pair].wait()
-        jacobian = jacobian_ref.at[pair]
-        done.append(chemistry(field, columns, jacobian, inverse_ref[:, columns], vector_ref))
+        if pair < far:
+            copies[pair].wait()
+            jacobian = jacobian_ref.at[pair]
+        else:
+            jacobian = jacobian_near_ref.at[pair - far]
+        done[pair] = chemistry(field, columns, jacobian, inverse_ref[:, columns], vector_ref)
     changed = from_species(done, turn_ref, depth).reshape(CELLS, CELLS, width)
     sources_ref[...] = changed
     sources = [changed[k] for k in range(CELLS)]
-    blank = jnp.zeros_like(left)
+    packed = packed_x_ref[...]
     put_rows(
         send_ref,
         [
             total([ends_x_ref[0, k] for k in range(CELLS)], sources),
             total([ends_x_ref[1, k] for k in range(CELLS)], sources),
-            *(transfer_ref[k] for k in range(4)),
-            blank,
-            blank,
+            packed,
+            jnp.zeros_like(packed),
         ],
     )
 
@@ -423,16 +454,16 @@
     return lax.all_to_all(blocks, axis, 0, 0, tiled=True).reshape(rows.shape)
 
 
-def solve_lines(send, axis):
+def solve_lines(send, scale, axis, depth):
     blocks = lax.axis_size(axis)
     tiles = send.shape[0] // (blocks * ROWS)
     states = pltpu.VMEM((tiles, blocks + CELLS, LANES), jnp.float32)
     terms = pltpu.VMEM((tiles, blocks, LANES), jnp.float32)
     ends = call(
-        functools.partial(solve_kernel, blocks, tiles),
+        functools.partial(solve_kernel, depth, axis, blocks, tiles),
         struct(2 * blocks * tiles, LANES),
-        [states] * 4 + [terms] * 4 + [states] * 2,
-    )(exchange(send, axis))
+        [states] * 4 + [terms] * 4 + [states] * 2 + [terms] * 4,
+    )(exchange(send, axis), scale)
     return exchange(ends, axis)
 
 
@@ -449,9 +480,9 @@
     block = struct(CELLS, CELLS, width)
     send = struct(CELLS * (width // LANES) * ROWS, LANES)
 
-    send_y = call(
+    send_y, scale = call(
         functools.partial(start_kernel, depth),
-        send,
+        [send, struct(CELLS, LANES)],
         [
             pltpu.VMEM(cotangent.shape, jnp.float32),
             pltpu.VMEM(conductance.shape, jnp.float32),
@@ -460,16 +491,19 @@
         ],
         far_in=(0, 1, 2),
     )(cotangent, conductance, diffusivity)
-    jacobian, inverse, local_y, ends_y, ends_x, sweep_x, transfer = call(
+    count = columns // LANES
+    tile = (species * species, LANES)
+    jacobian, jacobian_near, inverse, local_y, ends_y, ends_x, sweep_x, packed_x = call(
         functools.partial(prepare_kernel, depth),
         [
-            pltpu.HBM((columns // LANES, species * species, LANES), jnp.float32),
+            pltpu.HBM((count - NEAR, *tile), jnp.float32),
+            struct(NEAR, *tile),
             struct(species, columns),
             block,
             struct(2, CELLS, CELLS, width),
             struct(2, CELLS, CELLS, width),
             struct(5, CELLS, CELLS, width),
-            struct(4, CELLS, width),
+            struct(CELLS, LANES),
         ],
         [
             pltpu.VMEM(cotangent.shape, jnp.float32),
@@ -482,9 +516,9 @@
             turn,
             pltpu.VMEM((2 * reactions, columns), jnp.bfloat16),
             pltpu.VMEM((species * species, 2 * reactions), jnp.bfloat16),
-            pltpu.VMEM((columns // LANES, species * species, LANES), jnp.float32),
+            pltpu.VMEM((count - NEAR, *tile), jnp.float32),
             pltpu.SemaphoreType.DMA((7,)),
-            pltpu.SemaphoreType.DMA((columns // (2 * LANES),)),
+            pltpu.SemaphoreType.DMA((count - NEAR,)),
         ],
         far_in=tuple(range(7)),
         far_out=(0,),
@@ -497,19 +531,19 @@
         reactants.T,
         products.T,
     )
-    got_y = solve_lines(send_y, "gy")
+    got_y = solve_lines(send_y, scale, "gy", depth)
     send_x, sources = call(
         functools.partial(middle_kernel, depth),
         [send, block],
         [
             turn,
             pltpu.VMEM((species, columns), jnp.float32),
-            pltpu.VMEM((columns // LANES, species * species, LANES), jnp.float32),
-            pltpu.SemaphoreType.DMA((columns // LANES,)),
+            pltpu.VMEM((count - NEAR, *tile), jnp.float32),
+            pltpu.SemaphoreType.DMA((count - NEAR,)),
         ],
         far_in=(3,),
-    )(got_y, local_y, ends_y, jacobian, inverse, ends_x, transfer)
-    got_x = solve_lines(send_x, "gx")
+    )(got_y, local_y, ends_y, jacobian, jacobian_near, inverse, ends_x, packed_x)
+    got_x = solve_lines(send_x, scale, "gx", depth)
     return call(finish_kernel, block)(got_x, sources, sweep_x)
 
 

time: 68.9 us -> 66.7 us (0.968)
  blocking collectives: 51.8 us -> 50 us
    all_to_all x3, blocking collectives: 51.8 us -> 50 us  [exchange(): return lax.all_to_all(blocks, axis, 0, 0, tiled=True).reshape(rows.shape)]
where the time goes in v5:
time: 66.7 us; the launch traced here: 66.4 us
  blocking collectives  50 us (75%)
  Pallas kernels  9.27 us (14%)
  waiting for transfers between devices  3.6 us (5%)
  starting transfers between devices  3.5 us (5%)
    all_to_all x3, blocking collectives, exchange(): return lax.all_to_all(blocks, axis, 0, 0, tiled=True).reshape(rows.shape)  50 us
    pallas_call x6, Pallas kernels, run(): pl.pallas_call(kernel, out_shape=out_shape, in_specs=[far if k in far_in...  9.27 us
    all_to_all x1, waiting for transfers between devices, exchange(): return lax.all_to_all(blocks, axis, 0, 0, tiled=True).reshape(rows.shape)  3.6 us
    all_to_all x1, starting transfers between devices, exchange(): return lax.all_to_all(blocks, axis, 0, 0, tiled=True).reshape(rows.shape)  3.5 us
  transfers between devices with their start and end apart: 1, of which 1 were waited for; matrix products, arithmetic and copies ran while one was open for 0% of the time, Pallas kernels for 6%

profile of v5, /device:TPU:8, one launch (start us, length us, event | category | flops | bytes accessed | tf_op | source)
XLA Modules:
  0.0 66.4 jit_solution(5783592861968216894)
XLA Ops:
  0.0 1.2 %shard_map.73 = (f32[128,128]{1,0:T(8,128)S(1)}, f32[8,128]{1,0:T(8,128)S(1)}) custom-call(f32[8,8,512]{2,1,0:T(8,128)} %cot_from.3, f32[8,8,16]{2,1,0:T(8,128)} %cond_from.3, f32[1,32]{1,0:T(1,128)} %bitcast.21), custom_call_target="tpu_custom_call" | custom-call | tf_op jit(solution)/shard_map/pallas_call | solution.py:30
  1.2 18.0 %all_to_all.20 = f32[16,8,128]{2,1,0:T(8,128)S(1)} all-to-all(f32[16,8,128]{2,1,0:T(8,128)S(1)} %bitcast.18), channel_id=1, replica_groups=mesh['gx'=32,'gy'=16] {'gy'}, dimensions={0} | all-to-all | bytes 131072 | tf_op jit(solution)/shard_map/all_to_all | solution.py:454
  19.2 0.9 %shard_map.74 = f32[64,128]{1,0:T(8,128)} custom-call(f32[128,128]{1,0:T(8,128)S(1)} %bitcast.12, f32[8,128]{1,0:T(8,128)S(1)} %get-tuple-element.18.scale_ref), custom_call_target="tpu_custom_call" | custom-call | tf_op jit(solution)/shard_map/pallas_call | solution.py:30
  20.1 3.5 %all-to-all-start.1 = ((f32[16,4,128]{2,1,0:T(4,128)}), f32[16,4,128]{2,1,0:T(4,128)S(1)}, u32[]{:S(2)}, u32[]{:S(2)}) async-start(f32[16,4,128]{2,1,0:T(4,128)} %bitcast.3), calls=%async_computation.1 | async-start | bytes 65536 | tf_op jit(solution)/shard_map/all_to_all | solution.py:454
  23.6 4.1 %shard_map.75 = (f32[5,1024,128]{2,1,0:T(8,128)}, f32[3,1024,128]{2,1,0:T(8,128)S(1)}, f32[32,1024]{1,0:T(8,128)S(1)}, f32[8,8,512]{2,1,0:T(8,128)S(1)}, f32[2,8...) custom-call(f32[8,8,512]{2,1,0:T(8,128)} %cot_from.3, ...), custom_call_target="tpu_custom_call" | custom-call | tf_op jit(solution)/shard_map/pallas_call | solution.py:30
  27.6 3.6 %all-to-all-done.1 = f32[16,4,128]{2,1,0:T(4,128)S(1)} async-done(((f32[16,4,128]{2,1,0:T(4,128)}), f32[16,4,128]{2,1,0:T(4,128)S(1)}, u32[]{:S(2)}, u32[]{:S(2)}) %all-to-all-start.1) | async-done | bytes 32800 | tf_op jit(solution)/shard_map/all_to_all | solution.py:454
  31.2 2.2 %shard_map.76 = (f32[128,128]{1,0:T(8,128)S(1)}, f32[8,8,512]{2,1,0:T(8,128)S(1)}) custom-call(f32[64,128]{1,0:T(8,128)S(1)} %bitcast.14, f32[8,8,512]{2,1,0:T(8,128)S(1)} %get-tuple-element.19.local_ref, f32[2,8,8,512]{3,2,1,0:T(8,128)S(1)} %get-tuple-element.20.ends_y_ref, f32[5,1024,128]{2,1,0:T(8,128)} %get-tuple-element.21.jacobian_from, ...), custom_call_target="tpu_custom_call" | custom-call | tf_op jit(solution)/shard_map/pallas_call | solution.py:30
  33.4 19.1 %all_to_all.21 = f32[32,4,128]{2,1,0:T(4,128)S(1)} all-to-all(f32[32,4,128]{2,1,0:T(4,128)S(1)} %bitcast.17), channel_id=1, replica_groups=mesh['gx'=32,'gy'=16] {'gx'}, dimensions={0} | all-to-all | bytes 131072 | tf_op jit(solution)/shard_map/all_to_all | solution.py:454
  52.5 0.3 shard_map.77
  52.8 12.9 %all_to_all.22 = f32[32,2,128]{2,1,0:T(2,128)S(1)} all-to-all(f32[32,2,128]{2,1,0:T(2,128)S(1)} %bitcast.15), channel_id=1, replica_groups=mesh['gx'=32,'gy'=16] {'gx'}, dimensions={0} | all-to-all | bytes 65536 | tf_op jit(solution)/shard_map/all_to_all | solution.py:454
  65.7 0.7 %shard_map.78 = f32[8,8,512]{2,1,0:T(8,128)} custom-call(f32[64,128]{1,0:T(8,128)S(1)} %bitcast.16, f32[8,8,512]{2,1,0:T(8,128)S(1)} %get-tuple-element.27.sources_ref, f32[5,8,8,512]{3,2,1,0:T(8,128)S(1)} %get-tuple-element.28.sweep_ref), custom_call_target="tpu_custom_call" | custom-call | tf_op jit(solution)/shard_map/pallas_call | solution.py:30
Async XLA Ops:
  20.1 11.2 %all-to-all-start.1 = ((f32[16,4,128]{2,1,0:T(4,128)}), f32[16,4,128]{2,1,0:T(4,128)S(1)}, u32[]{:S(2)}, u32[]{:S(2)}) async-start(f32[16,4,128]{2,1,0:T(4,128)} %bitcast.3), calls=%async_computation.1 | async-start | bytes 65536 | tf_op jit(solution)/shard_map/all_to_all | solution.py:454

commit v6 on v5

--- a/solution.py
+++ b/solution.py
@@ -11,7 +11,7 @@
 CELLS = 8
 LANES = 128
 ROWS = 4
-NEAR = 3
+NEAR = 5
 LIMIT = 16 << 20
 
 
@@ -50,29 +50,28 @@
     return copies
 
 
+def copied(values, source_of, width):
+    high = values.astype(jnp.bfloat16)
+    rest = values - high.astype(jnp.float32)
+    middle = rest.astype(jnp.bfloat16)
+    low = (rest - middle.astype(jnp.float32)).astype(jnp.bfloat16)
+    count = values.shape[1]
+    lane = lax.broadcasted_iota(jnp.int32, (3 * count, width), 1)
+    row = lax.broadcasted_iota(jnp.int32, (3 * count, width), 0)
+    same = (source_of(lane) == lax.rem(row, count)).astype(jnp.bfloat16)
+    parts = jnp.concatenate([high, middle, low], axis=1)
+    return jnp.dot(parts, same, preferred_element_type=jnp.float32)
+
+
 def species_scale(diffusivity, width, depth):
-    species = width // depth
-    lane = lax.broadcasted_iota(jnp.int32, (species, width), 1)
-    same = lax.div(lane, depth) == lax.broadcasted_iota(jnp.int32, (species, width), 0)
-    return jnp.dot(
-        jnp.broadcast_to(1.0 / diffusivity, (CELLS, species)),
-        same.astype(jnp.float32),
-        precision=lax.Precision.HIGHEST,
-        preferred_element_type=jnp.float32,
-    )
+    inverse = jnp.broadcast_to(1.0 / diffusivity, (2 * CELLS, width // depth))
+    return copied(inverse, lambda lane: lax.div(lane, depth), width)[:CELLS]
 
 
 def cell_rates(cond, scale, depth):
     width = scale.shape[1]
-    lane = lax.broadcasted_iota(jnp.int32, (depth, width), 1)
-    same = lax.rem(lane, depth) == lax.broadcasted_iota(jnp.int32, (depth, width), 0)
-    spread = jnp.dot(
-        (1.0 / cond).reshape(-1, depth),
-        same.astype(jnp.float32),
-        precision=lax.Precision.HIGHEST,
-        preferred_element_type=jnp.float32,
-    )
-    tiles = spread.reshape(CELLS, CELLS, width)
+    inverse = (1.0 / cond).reshape(-1, depth)
+    tiles = copied(inverse, lambda lane: lax.rem(lane, depth), width).reshape(CELLS, CELLS, width)
     return [tiles[cell] * scale for cell in range(CELLS)]
 
 
@@ -297,9 +296,10 @@
 
 def prepare_kernel(
     depth, cot_from, conc_from, cond_from, diffusivity_from, rate_from, reactants_from,
-    products_from, jacobian_to, jacobian_near_ref, inverse_ref, local_y_ref, ends_y_ref,
-    ends_x_ref, sweep_x_ref, packed_x_ref, cot_ref, conc_ref, cond_ref, diffusivity_ref, rate_ref, reactants_ref,
-    products_ref, turn_ref, rates_ref, pairs_ref, jacobian_ref, in_sem, sem,
+    products_from, jacobian_to, sweep_x_to, jacobian_near_ref, local_y_ref, ends_y_ref,
+    ends_x_ref, packed_x_ref, cot_ref, conc_ref, cond_ref, diffusivity_ref, rate_ref,
+    reactants_ref, products_ref, turn_ref, rates_ref, pairs_ref, inverse_ref, sweep_x_ref,
+    jacobian_ref, in_sem, sem,
 ):
     inputs = begin(
         [
@@ -340,7 +340,9 @@
         block = jnp.dot(pairs_ref[...], rates_ref[:, columns], preferred_element_type=jnp.float32)
         for part in range(2):
             tile = 2 * chunk + part - jacobian_ref.shape[0]
-            value = block[:, part * LANES : (part + 1) * LANES]
+            here = pl.ds((2 * chunk + part) * LANES, LANES)
+            value = block[:, part * LANES : (part + 1) * LANES].reshape(species, species, LANES)
+            value = (value * inverse_ref[:, here][None]).reshape(-1, LANES)
             if tile >= 0:
                 jacobian_near_ref[tile] = value
                 continue
@@ -365,6 +367,10 @@
         sweep_x_ref[2, k] = gains[k] * rates[k]
         sweep_x_ref[3, k] = to_first[k] * rates[k]
         sweep_x_ref[4, k] = to_last[k] * rates[k]
+    copies.append(
+        pltpu.make_async_copy(sweep_x_ref, sweep_x_to, sem.at[jacobian_ref.shape[0]])
+    )
+    copies[-1].start()
     rates = cell_rates(jnp.swapaxes(cond, 0, 1), scale, depth)
     to_first, to_last = factors(rates)
     lines = jnp.swapaxes(cot_ref[...], 0, 1)
@@ -377,7 +383,7 @@
         copy.wait()
 
 
-def chemistry(field, columns, jacobian_ref, inverse, vector_ref):
+def chemistry(field, columns, jacobian_ref, vector_ref):
     species = field.shape[0]
 
     def transposed(vector):
@@ -387,7 +393,7 @@
             row = jnp.broadcast_to(vector_ref[pl.ds(s, 1), columns], vector.shape)
             term = row * jacobian_ref[pl.ds(s * species, species), :]
             sums[s % 4] = term if sums[s % 4] is None else sums[s % 4] + term
-        return ((sums[0] + sums[1]) + (sums[2] + sums[3])) * inverse
+        return (sums[0] + sums[1]) + (sums[2] + sums[3])
 
     third = field + transposed(field) * (1.0 / 3.0)
     second = field + transposed(third) * 0.5
@@ -395,13 +401,18 @@
 
 
 def middle_kernel(
-    depth, ends_ref, local_ref, ends_y_ref, jacobian_from, jacobian_near_ref, inverse_ref,
-    ends_x_ref, packed_x_ref, send_ref, sources_ref, turn_ref, vector_ref, jacobian_ref, sem,
+    depth, ends_ref, local_ref, ends_y_ref, jacobian_from, jacobian_near_ref, ends_x_ref,
+    packed_x_ref, sweep_from, send_ref, sources_ref, sweep_ref, turn_ref, vector_ref,
+    jacobian_ref, sem,
 ):
     width = local_ref.shape[2]
     far = jacobian_ref.shape[0]
     copies = begin(
-        [(jacobian_from.at[tile], jacobian_ref.at[tile]) for tile in range(far)], sem
+        [
+            *((jacobian_from.at[tile], jacobian_ref.at[tile]) for tile in range(far)),
+            (sweep_from, sweep_ref),
+        ],
+        sem,
     )
     left, right = get_ends(ends_ref)
     solved = jnp.stack(
@@ -422,7 +433,7 @@
             jacobian = jacobian_ref.at[pair]
         else:
             jacobian = jacobian_near_ref.at[pair - far]
-        done[pair] = chemistry(field, columns, jacobian, inverse_ref[:, columns], vector_ref)
+        done[pair] = chemistry(field, columns, jacobian, vector_ref)
     changed = from_species(done, turn_ref, depth).reshape(CELLS, CELLS, width)
     sources_ref[...] = changed
     sources = [changed[k] for k in range(CELLS)]
@@ -436,6 +447,7 @@
             jnp.zeros_like(packed),
         ],
     )
+    copies[far].wait()
 
 
 def finish_kernel(ends_ref, sources_ref, sweep_ref, out_ref):
@@ -493,16 +505,16 @@
     )(cotangent, conductance, diffusivity)
     count = columns // LANES
     tile = (species * species, LANES)
-    jacobian, jacobian_near, inverse, local_y, ends_y, ends_x, sweep_x, packed_x = call(
+    sweep = (5, CELLS, CELLS, width)
+    jacobian, sweep_x, jacobian_near, local_y, ends_y, ends_x, packed_x = call(
         functools.partial(prepare_kernel, depth),
         [
             pltpu.HBM((count - NEAR, *tile), jnp.float32),
+            pltpu.HBM(sweep, jnp.float32),
             struct(NEAR, *tile),
-            struct(species, columns),
             block,
             struct(2, CELLS, CELLS, width),
             struct(2, CELLS, CELLS, width),
-            struct(5, CELLS, CELLS, width),
             struct(CELLS, LANES),
         ],
         [
@@ -516,12 +528,14 @@
             turn,
             pltpu.VMEM((2 * reactions, columns), jnp.bfloat16),
             pltpu.VMEM((species * species, 2 * reactions), jnp.bfloat16),
+            pltpu.VMEM((species, columns), jnp.float32),
+            pltpu.VMEM(sweep, jnp.float32),
             pltpu.VMEM((count - NEAR, *tile), jnp.float32),
             pltpu.SemaphoreType.DMA((7,)),
-            pltpu.SemaphoreType.DMA((count - NEAR,)),
+            pltpu.SemaphoreType.DMA((count - NEAR + 1,)),
         ],
         far_in=tuple(range(7)),
-        far_out=(0,),
+        far_out=(0, 1),
     )(
         cotangent,
         concentration,
@@ -532,17 +546,17 @@
         products.T,
     )
     got_y = solve_lines(send_y, scale, "gy", depth)
-    send_x, sources = call(
+    send_x, sources, sweep_x = call(
         functools.partial(middle_kernel, depth),
-        [send, block],
+        [send, block, struct(*sweep)],
         [
             turn,
             pltpu.VMEM((species, columns), jnp.float32),
             pltpu.VMEM((count - NEAR, *tile), jnp.float32),
-            pltpu.SemaphoreType.DMA((count - NEAR,)),
-        ],
-        far_in=(3,),
-    )(got_y, local_y, ends_y, jacobian, jacobian_near, inverse, ends_x, packed_x)
+            pltpu.SemaphoreType.DMA((count - NEAR + 1,)),
+        ],
+        far_in=(3, 7),
+    )(got_y, local_y, ends_y, jacobian, jacobian_near, ends_x, packed_x, sweep_x)
     got_x = solve_lines(send_x, scale, "gx", depth)
     return call(finish_kernel, block)(got_x, sources, sweep_x)
 

time: 66.7 us -> 66.3 us (level)
  no operation moved by 1% of the time
where the time goes in v6:
time: 66.3 us; the launch traced here: 65.9 us
  blocking collectives  50 us (75%)
  Pallas kernels  8.87 us (13%)
  waiting for transfers between devices  3.58 us (5%)
  starting transfers between devices  3.5 us (5%)
    all_to_all x3, blocking collectives, exchange(): return lax.all_to_all(blocks, axis, 0, 0, tiled=True).reshape(rows.shape)  50 us
    pallas_call x6, Pallas kernels, run(): pl.pallas_call(kernel, out_shape=out_shape, in_specs=[far if k in far_in...  8.87 us
    all_to_all x1, waiting for transfers between devices, exchange(): return lax.all_to_all(blocks, axis, 0, 0, tiled=True).reshape(rows.shape)  3.58 us
    all_to_all x1, starting transfers between devices, exchange(): return lax.all_to_all(blocks, axis, 0, 0, tiled=True).reshape(rows.shape)  3.5 us
  transfers between devices with their start and end apart: 1, of which 1 were waited for; matrix products, arithmetic and copies ran while one was open for 0% of the time, Pallas kernels for 6%

profile of v6, /device:TPU:8, one launch (start us, length us, event | category | flops | bytes accessed | tf_op | source)
XLA Modules:
  0.0 65.9 jit_solution(10786454544902620898)
XLA Ops:
  0.0 1.1 %shard_map.73 = (f32[128,128]{1,0:T(8,128)S(1)}, f32[8,128]{1,0:T(8,128)S(1)}) custom-call(f32[8,8,512]{2,1,0:T(8,128)} %cot_from.3, f32[8,8,16]{2,1,0:T(8,128)} %cond_from.3, f32[1,32]{1,0:T(1,128)} %bitcast.21), custom_call_target="tpu_custom_call" | custom-call | tf_op jit(solution)/shard_map/pallas_call | solution.py:30
  1.1 18.0 %all_to_all.20 = f32[16,8,128]{2,1,0:T(8,128)S(1)} all-to-all(f32[16,8,128]{2,1,0:T(8,128)S(1)} %bitcast.18), channel_id=1, replica_groups=mesh['gx'=32,'gy'=16] {'gy'}, dimensions={0} | all-to-all | bytes 131072 | tf_op jit(solution)/shard_map/all_to_all | solution.py:466
  19.1 0.9 %shard_map.74 = f32[64,128]{1,0:T(8,128)} custom-call(f32[128,128]{1,0:T(8,128)S(1)} %bitcast.12, f32[8,128]{1,0:T(8,128)S(1)} %get-tuple-element.18.scale_ref), custom_call_target="tpu_custom_call" | custom-call | tf_op jit(solution)/shard_map/pallas_call | solution.py:30
  20.0 3.5 %all-to-all-start.1 = ((f32[16,4,128]{2,1,0:T(4,128)}), f32[16,4,128]{2,1,0:T(4,128)S(1)}, u32[]{:S(2)}, u32[]{:S(2)}) async-start(f32[16,4,128]{2,1,0:T(4,128)} %bitcast.3), calls=%async_computation.1 | async-start | bytes 65536 | tf_op jit(solution)/shard_map/all_to_all | solution.py:466
  23.5 4.1 %shard_map.75 = (f32[3,1024,128]{2,1,0:T(8,128)}, f32[5,8,8,512]{3,2,1,0:T(8,128)}, f32[5,1024,128]{2,1,0:T(8,128)S(1)}, f32[8,8,512]{2,1,0:T(8,128)S(1)}, f32[2...) custom-call(f32[8,8,512]{2,1,0:T(8,128)} %cot_from.3, f32[8,8,512]{2,1,0:T(8,128)} %conc_from.1, ...), custom_call_target="tpu_custom_call" | custom-call | tf_op jit(solution)/shard_map/pallas_call | solution.py:30
  27.6 3.6 %all-to-all-done.1 = f32[16,4,128]{2,1,0:T(4,128)S(1)} async-done(((f32[16,4,128]{2,1,0:T(4,128)}), f32[16,4,128]{2,1,0:T(4,128)S(1)}, u32[]{:S(2)}, u32[]{:S(2)}) %all-to-all-start.1) | async-done | bytes 32800 | tf_op jit(solution)/shard_map/all_to_all | solution.py:466
  31.2 1.8 %shard_map.76 = (f32[128,128]{1,0:T(8,128)S(1)}, f32[8,8,512]{2,1,0:T(8,128)S(1)}, f32[5,8,8,512]{3,2,1,0:T(8,128)S(1)}) custom-call(f32[64,128]{1,0:T(8,128)S(1)} %bitcast.14, f32[8,8,512]{2,1,0:T(8,128)S(1)} %get-tuple-element.19.local_ref, f32[2,8,8,512]{3,2,1,0:T(8,128)S(1)} %get-tuple-element.20.ends_y_ref, ...), custom_call_target="tpu_custom_call" | custom-call | tf_op jit(solution)/shard_map/pallas_call | solution.py:30
  33.0 19.1 %all_to_all.21 = f32[32,4,128]{2,1,0:T(4,128)S(1)} all-to-all(f32[32,4,128]{2,1,0:T(4,128)S(1)} %bitcast.17), channel_id=1, replica_groups=mesh['gx'=32,'gy'=16] {'gx'}, dimensions={0} | all-to-all | bytes 131072 | tf_op jit(solution)/shard_map/all_to_all | solution.py:466
  52.1 0.3 shard_map.77
  52.4 12.9 %all_to_all.22 = f32[32,2,128]{2,1,0:T(2,128)S(1)} all-to-all(f32[32,2,128]{2,1,0:T(2,128)S(1)} %bitcast.15), channel_id=1, replica_groups=mesh['gx'=32,'gy'=16] {'gx'}, dimensions={0} | all-to-all | bytes 65536 | tf_op jit(solution)/shard_map/all_to_all | solution.py:466
  65.2 0.7 %shard_map.78 = f32[8,8,512]{2,1,0:T(8,128)} custom-call(f32[64,128]{1,0:T(8,128)S(1)} %bitcast.16, f32[8,8,512]{2,1,0:T(8,128)S(1)} %get-tuple-element.27.sources_ref, f32[5,8,8,512]{3,2,1,0:T(8,128)S(1)} %get-tuple-element.28.sweep_ref), custom_call_target="tpu_custom_call" | custom-call | tf_op jit(solution)/shard_map/pallas_call | solution.py:30
Async XLA Ops:
  20.0 11.2 %all-to-all-start.1 = ((f32[16,4,128]{2,1,0:T(4,128)}), f32[16,4,128]{2,1,0:T(4,128)S(1)}, u32[]{:S(2)}, u32[]{:S(2)}) async-start(f32[16,4,128]{2,1,0:T(4,128)} %bitcast.3), calls=%async_computation.1 | async-start | bytes 65536 | tf_op jit(solution)/shard_map/all_to_all | solution.py:466

commit v7 on v6

--- a/solution.py
+++ b/solution.py
@@ -92,26 +92,18 @@
     return [value * inverse for value in right], [value * inverse for value in left]
 
 
-def sweep_factors(to_first, to_last):
-    ratio = to_last[0] * 0.0
-    forward = [to_last[k] / to_last[k + 1] for k in range(CELLS - 1)] + [ratio]
-    backward = [ratio] + [to_first[k] / to_first[k - 1] for k in range(1, CELLS)]
+def local_solution(sources, to_first, to_last):
     scale = 1.0 / to_first[CELLS - 1]
-    gains = [to_first[k] * to_last[k] * scale for k in range(CELLS)]
-    return forward, backward, gains
-
-
-def local_solution(sources, forward, backward, gains):
     before, after = [None] * CELLS, [None] * CELLS
-    running = sources[0] * 0.0
+    running = to_last[0] * sources[0]
     for k in range(CELLS):
-        before[k] = sources[k] + running
-        running = forward[k] * before[k]
-    running = sources[0] * 0.0
+        running = running if k == 0 else running + to_last[k] * sources[k]
+        before[k] = running
+    running = jnp.zeros_like(scale)
     for k in reversed(range(CELLS)):
         after[k] = running
-        running = backward[k] * (sources[k] + running)
-    return [(before[k] + after[k]) * gains[k] for k in range(CELLS)]
+        running = running + to_first[k] * sources[k]
+    return [(to_first[k] * before[k] + to_last[k] * after[k]) * scale for k in range(CELLS)]
 
 
 def total(weights, sources):
@@ -149,7 +141,12 @@
 ):
     width = cot_ref.shape[2]
     copies = begin(
-        [(cond_from, cond_ref), (diffusivity_from, diffusivity_ref), (cot_from, cot_ref)], sem
+        [
+            (cond_from, cond_ref),
+            (diffusivity_from, diffusivity_ref),
+            *((cot_from.at[pl.ds(k, 2)], cot_ref.at[pl.ds(k, 2)]) for k in range(0, CELLS, 2)),
+        ],
+        sem,
     )
     copies[0].wait()
     copies[1].wait()
@@ -159,7 +156,8 @@
     packed = pack(cond)
     for tile in range(4):
         scale_ref[pl.ds(tile, 1), :] = scale[0:1, tile * LANES : (tile + 1) * LANES]
-    copies[2].wait()
+    for copy in copies[2:]:
+        copy.wait()
     lines = jnp.swapaxes(cot_ref[...], 0, 1)
     sources = [lines[cell] for cell in range(CELLS)]
     put_rows(
@@ -296,10 +294,10 @@
 
 def prepare_kernel(
     depth, cot_from, conc_from, cond_from, diffusivity_from, rate_from, reactants_from,
-    products_from, jacobian_to, sweep_x_to, jacobian_near_ref, local_y_ref, ends_y_ref,
-    ends_x_ref, packed_x_ref, cot_ref, conc_ref, cond_ref, diffusivity_ref, rate_ref,
-    reactants_ref, products_ref, turn_ref, rates_ref, pairs_ref, inverse_ref, sweep_x_ref,
-    jacobian_ref, in_sem, sem,
+    products_from, jacobian_to, jacobian_near_ref, local_y_ref, ends_y_ref, ends_x_ref,
+    rates_x_ref, packed_x_ref, cot_ref, conc_ref, cond_ref, diffusivity_ref, rate_ref,
+    reactants_ref, products_ref, turn_ref, rates_ref, pairs_ref, inverse_ref, jacobian_ref,
+    in_sem, sem,
 ):
     inputs = begin(
         [
@@ -358,23 +356,14 @@
     packed_x_ref[...] = pack(cond)
     rates = cell_rates(cond, scale, depth)
     to_first, to_last = factors(rates)
-    forward, backward, gains = sweep_factors(to_first, to_last)
     for k in range(CELLS):
         ends_x_ref[0, k] = to_first[k]
         ends_x_ref[1, k] = to_last[k]
-        sweep_x_ref[0, k] = forward[k]
-        sweep_x_ref[1, k] = backward[k]
-        sweep_x_ref[2, k] = gains[k] * rates[k]
-        sweep_x_ref[3, k] = to_first[k] * rates[k]
-        sweep_x_ref[4, k] = to_last[k] * rates[k]
-    copies.append(
-        pltpu.make_async_copy(sweep_x_ref, sweep_x_to, sem.at[jacobian_ref.shape[0]])
-    )
-    copies[-1].start()
+        rates_x_ref[k] = rates[k]
     rates = cell_rates(jnp.swapaxes(cond, 0, 1), scale, depth)
     to_first, to_last = factors(rates)
     lines = jnp.swapaxes(cot_ref[...], 0, 1)
-    local = local_solution([lines[k] for k in range(CELLS)], *sweep_factors(to_first, to_last))
+    local = local_solution([lines[k] for k in range(CELLS)], to_first, to_last)
     for k in range(CELLS):
         local_y_ref[k] = local[k] * rates[k]
         ends_y_ref[0, k] = to_first[k] * rates[k]
@@ -402,17 +391,12 @@
 
 def middle_kernel(
     depth, ends_ref, local_ref, ends_y_ref, jacobian_from, jacobian_near_ref, ends_x_ref,
-    packed_x_ref, sweep_from, send_ref, sources_ref, sweep_ref, turn_ref, vector_ref,
-    jacobian_ref, sem,
+    packed_x_ref, send_ref, sources_ref, turn_ref, vector_ref, jacobian_ref, sem,
 ):
     width = local_ref.shape[2]
     far = jacobian_ref.shape[0]
     copies = begin(
-        [
-            *((jacobian_from.at[tile], jacobian_ref.at[tile]) for tile in range(far)),
-            (sweep_from, sweep_ref),
-        ],
-        sem,
+        [(jacobian_from.at[tile], jacobian_ref.at[tile]) for tile in range(far)], sem
     )
     left, right = get_ends(ends_ref)
     solved = jnp.stack(
@@ -447,17 +431,22 @@
             jnp.zeros_like(packed),
         ],
     )
-    copies[far].wait()
-
-
-def finish_kernel(ends_ref, sources_ref, sweep_ref, out_ref):
-    local = local_solution(
-        [sources_ref[k] for k in range(CELLS)],
-        *([sweep_ref[part, k] for k in range(CELLS)] for part in range(3)),
-    )
+
+
+def finish_kernel(ends_ref, sources_ref, ends_x_ref, rates_ref, out_to, out_ref, sem):
+    to_first = [ends_x_ref[0, k] for k in range(CELLS)]
+    to_last = [ends_x_ref[1, k] for k in range(CELLS)]
+    local = local_solution([sources_ref[k] for k in range(CELLS)], to_first, to_last)
     left, right = get_ends(ends_ref)
+    copies = []
     for k in range(CELLS):
-        out_ref[k] = local[k] + sweep_ref[3, k] * left + sweep_ref[4, k] * right
+        out_ref[k] = (local[k] + to_first[k] * left + to_last[k] * right) * rates_ref[k]
+        if k % 2:
+            pair = pl.ds(k - 1, 2)
+            copies.append(pltpu.make_async_copy(out_ref.at[pair], out_to.at[pair], sem.at[k // 2]))
+            copies[-1].start()
+    for copy in copies:
+        copy.wait()
 
 
 def exchange(rows, axis):
@@ -499,22 +488,21 @@
             pltpu.VMEM(cotangent.shape, jnp.float32),
             pltpu.VMEM(conductance.shape, jnp.float32),
             pltpu.VMEM(diffusivity.shape, jnp.float32),
-            pltpu.SemaphoreType.DMA((3,)),
+            pltpu.SemaphoreType.DMA((6,)),
         ],
         far_in=(0, 1, 2),
     )(cotangent, conductance, diffusivity)
     count = columns // LANES
     tile = (species * species, LANES)
-    sweep = (5, CELLS, CELLS, width)
-    jacobian, sweep_x, jacobian_near, local_y, ends_y, ends_x, packed_x = call(
+    jacobian, jacobian_near, local_y, ends_y, ends_x, rates_x, packed_x = call(
         functools.partial(prepare_kernel, depth),
         [
             pltpu.HBM((count - NEAR, *tile), jnp.float32),
-            pltpu.HBM(sweep, jnp.float32),
             struct(NEAR, *tile),
             block,
             struct(2, CELLS, CELLS, width),
             struct(2, CELLS, CELLS, width),
+            block,
             struct(CELLS, LANES),
         ],
         [
@@ -529,13 +517,12 @@
             pltpu.VMEM((2 * reactions, columns), jnp.bfloat16),
             pltpu.VMEM((species * species, 2 * reactions), jnp.bfloat16),
             pltpu.VMEM((species, columns), jnp.float32),
-            pltpu.VMEM(sweep, jnp.float32),
             pltpu.VMEM((count - NEAR, *tile), jnp.float32),
             pltpu.SemaphoreType.DMA((7,)),
-            pltpu.SemaphoreType.DMA((count - NEAR + 1,)),
+            pltpu.SemaphoreType.DMA((count - NEAR,)),
         ],
         far_in=tuple(range(7)),
-        far_out=(0, 1),
+        far_out=(0,),
     )(
         cotangent,
         concentration,
@@ -546,19 +533,24 @@
         products.T,
     )
     got_y = solve_lines(send_y, scale, "gy", depth)
-    send_x, sources, sweep_x = call(
+    send_x, sources = call(
         functools.partial(middle_kernel, depth),
-        [send, block, struct(*sweep)],
+        [send, block],
         [
             turn,
             pltpu.VMEM((species, columns), jnp.float32),
             pltpu.VMEM((count - NEAR, *tile), jnp.float32),
-            pltpu.SemaphoreType.DMA((count - NEAR + 1,)),
-        ],
-        far_in=(3, 7),
-    )(got_y, local_y, ends_y, jacobian, jacobian_near, ends_x, packed_x, sweep_x)
+            pltpu.SemaphoreType.DMA((count - NEAR,)),
+        ],
+        far_in=(3,),
+    )(got_y, local_y, ends_y, jacobian, jacobian_near, ends_x, packed_x)
     got_x = solve_lines(send_x, scale, "gx", depth)
-    return call(finish_kernel, block)(got_x, sources, sweep_x)
+    return call(
+        finish_kernel,
+        [block],
+        [pltpu.VMEM(block.shape, jnp.float32), pltpu.SemaphoreType.DMA((CELLS // 2,))],
+        far_out=(0,),
+    )(got_x, sources, ends_x, rates_x)[0]
 
 
 def solution(mesh):

time: 66.3 us -> 66.4 us (level)
  no operation moved by 1% of the time
where the time goes in v7:
time: 66.4 us; the launch traced here: 66 us
  blocking collectives  50 us (75%)
  Pallas kernels  8.63 us (13%)
  waiting for transfers between devices  3.86 us (6%)
  starting transfers between devices  3.5 us (5%)
    all_to_all x3, blocking collectives, exchange(): return lax.all_to_all(blocks, axis, 0, 0, tiled=True).reshape(rows.shape)  50 us
    pallas_call x6, Pallas kernels, run(): pl.pallas_call(kernel, out_shape=out_shape, in_specs=[far if k in far_in...  8.63 us
    all_to_all x1, waiting for transfers between devices, exchange(): return lax.all_to_all(blocks, axis, 0, 0, tiled=True).reshape(rows.shape)  3.86 us
    all_to_all x1, starting transfers between devices, exchange(): return lax.all_to_all(blocks, axis, 0, 0, tiled=True).reshape(rows.shape)  3.5 us
  transfers between devices with their start and end apart: 1, of which 1 were waited for; matrix products, arithmetic and copies ran while one was open for 0% of the time, Pallas kernels for 6%

profile of v7, /device:TPU:8, one launch (start us, length us, event | category | flops | bytes accessed | tf_op | source)
XLA Modules:
  0.0 66.0 jit_solution(7658971364698749713)
XLA Ops:
  0.0 1.1 %shard_map.73 = (f32[128,128]{1,0:T(8,128)S(1)}, f32[8,128]{1,0:T(8,128)S(1)}) custom-call(f32[8,8,512]{2,1,0:T(8,128)} %cot_from.3, f32[8,8,16]{2,1,0:T(8,128)} %cond_from.3, f32[1,32]{1,0:T(1,128)} %bitcast.21), custom_call_target="tpu_custom_call" | custom-call | tf_op jit(solution)/shard_map/pallas_call | solution.py:30
  1.1 18.0 %all_to_all.20 = f32[16,8,128]{2,1,0:T(8,128)S(1)} all-to-all(f32[16,8,128]{2,1,0:T(8,128)S(1)} %bitcast.18), channel_id=1, replica_groups=mesh['gx'=32,'gy'=16] {'gy'}, dimensions={0} | all-to-all | bytes 131072 | tf_op jit(solution)/shard_map/all_to_all | solution.py:455
  19.2 0.9 %shard_map.74 = f32[64,128]{1,0:T(8,128)} custom-call(f32[128,128]{1,0:T(8,128)S(1)} %bitcast.12, f32[8,128]{1,0:T(8,128)S(1)} %get-tuple-element.17.scale_ref), custom_call_target="tpu_custom_call" | custom-call | tf_op jit(solution)/shard_map/pallas_call | solution.py:30
  20.0 3.5 %all-to-all-start.1 = ((f32[16,4,128]{2,1,0:T(4,128)}), f32[16,4,128]{2,1,0:T(4,128)S(1)}, u32[]{:S(2)}, u32[]{:S(2)}) async-start(f32[16,4,128]{2,1,0:T(4,128)} %bitcast.3), calls=%async_computation.1 | async-start | bytes 65536 | tf_op jit(solution)/shard_map/all_to_all | solution.py:455
  23.5 3.8 %shard_map.75 = (f32[3,1024,128]{2,1,0:T(8,128)}, f32[5,1024,128]{2,1,0:T(8,128)S(1)}, f32[8,8,512]{2,1,0:T(8,128)S(1)}, f32[2,8,8,512]{3,2,1,0:T(8,128)S(1)}, f...) custom-call(f32[8,8,512]{2,1,0:T(8,128)} %cot_from.3, f32[8,8,512]{2,1,0:T(8,128)} %conc_from.1, ...), custom_call_target="tpu_custom_call" | custom-call | tf_op jit(solution)/shard_map/pallas_call | solution.py:30
  27.3 3.9 %all-to-all-done.1 = f32[16,4,128]{2,1,0:T(4,128)S(1)} async-done(((f32[16,4,128]{2,1,0:T(4,128)}), f32[16,4,128]{2,1,0:T(4,128)S(1)}, u32[]{:S(2)}, u32[]{:S(2)}) %all-to-all-start.1) | async-done | bytes 32800 | tf_op jit(solution)/shard_map/all_to_all | solution.py:455
  31.2 1.8 %shard_map.76 = (f32[128,128]{1,0:T(8,128)S(1)}, f32[8,8,512]{2,1,0:T(8,128)S(1)}) custom-call(f32[64,128]{1,0:T(8,128)S(1)} %bitcast.14, f32[8,8,512]{2,1,0:T(8,128)S(1)} %get-tuple-element.18.local_ref, f32[2,8,8,512]{3,2,1,0:T(8,128)S(1)} %get-tuple-element.19.ends_y_ref, f32[3,1024,128]{2,1,0:T(8,128)} %get-tuple-element.20.jacobian_from, ...), custom_call_target="tpu_custom_call" | custom-call | tf_op jit(solution)/shard_map/pallas_call | solution.py:30
  33.0 19.1 %all_to_all.21 = f32[32,4,128]{2,1,0:T(4,128)S(1)} all-to-all(f32[32,4,128]{2,1,0:T(4,128)S(1)} %bitcast.17), channel_id=1, replica_groups=mesh['gx'=32,'gy'=16] {'gx'}, dimensions={0} | all-to-all | bytes 131072 | tf_op jit(solution)/shard_map/all_to_all | solution.py:455
  52.1 0.3 shard_map.77
  52.4 12.9 %all_to_all.22 = f32[32,2,128]{2,1,0:T(2,128)S(1)} all-to-all(f32[32,2,128]{2,1,0:T(2,128)S(1)} %bitcast.15), channel_id=1, replica_groups=mesh['gx'=32,'gy'=16] {'gx'}, dimensions={0} | all-to-all | bytes 65536 | tf_op jit(solution)/shard_map/all_to_all | solution.py:455
  65.3 0.7 %shard_map.78 = f32[8,8,512]{2,1,0:T(8,128)} custom-call(f32[64,128]{1,0:T(8,128)S(1)} %bitcast.16, f32[8,8,512]{2,1,0:T(8,128)S(1)} %get-tuple-element.25.sources_ref, f32[2,8,8,512]{3,2,1,0:T(8,128)S(1)} %get-tuple-element.22.ends_x_ref, f32[8,8,512]{2,1,0:T(8,128)S(1)} %get-tuple-element.26.rates_ref), custom_call_target="tpu_custom_call" | custom-call | tf_op jit(solution)/shard_map/pallas_call | solution.py:30
Async XLA Ops:
  20.0 11.2 %all-to-all-start.1 = ((f32[16,4,128]{2,1,0:T(4,128)}), f32[16,4,128]{2,1,0:T(4,128)S(1)}, u32[]{:S(2)}, u32[]{:S(2)}) async-start(f32[16,4,128]{2,1,0:T(4,128)} %bitcast.3), calls=%async_computation.1 | async-start | bytes 65536 | tf_op jit(solution)/shard_map/all_to_all | solution.py:455

commit v8 on v7

--- a/solution.py
+++ b/solution.py
@@ -168,7 +168,9 @@
 
 def solve_kernel(depth, axis, blocks, tiles, got_ref, scale_ref, out_ref, *scratch):
     value_l, step_l, value_r, step_r, ratio_l, add_l, ratio_r, add_r, sum_l, sum_r = scratch[:10]
-    moves = scratch[10:]
+    moves, joined = scratch[10:14], scratch[14:]
+    pairs = blocks // 2
+    even, odd, after = (pl.ds(start, pairs, stride=2) for start in range(3))
     me = lax.axis_index(axis)
     one = jnp.ones((1, LANES), jnp.float32)
 
@@ -192,26 +194,44 @@
         last = CELLS - 1
         for move, value in zip(moves, (flat_step, slope_step, flat[last], slope[last]), strict=True):
             move[tile] = value
+        c0, d0, e0, f0 = (move[tile, even, :] for move in moves)
+        c1, d1, e1, f1 = (move[tile, odd, :] for move in moves)
+        a0, b0 = c0 + e0, d0 + f0
+        joined[0][tile] = c1 * a0 + d1 * c0
+        joined[1][tile] = c1 * b0 + d1 * d0
+        joined[2][tile] = e1 * a0 + f1 * c0
+        joined[3][tile] = e1 * b0 + f1 * d0
+
+    def onward(state, move):
+        value, step = state
+        c, d, e, f = move
+        following = c * value + d * step
+        return following + (e * value + f * step), following
+
+    lefts = [(one, one)] * tiles
+    rights = [(one, one)] * tiles
+    for pair in range(pairs):
+        mirror = pairs - 1 - pair
+        for tile in range(tiles):
+            left, right = lefts[tile], rights[tile]
+            value_l[tile, pl.ds(2 * pair, 1), :], step_l[tile, pl.ds(2 * pair, 1), :] = left
+            row = pl.ds(2 * mirror + 2, 1)
+            value_r[tile, row, :], step_r[tile, row, :] = right
+            c, d, e, f = (move[tile, pl.ds(pair, 1), :] for move in joined)
+            lefts[tile] = onward(left, (c, d, e, f))
+            c, d, e, f = (move[tile, pl.ds(mirror, 1), :] for move in joined)
+            rights[tile] = onward(right, (c, e, d, f))
     for tile in range(tiles):
-        left, left_step, right, right_step = one, one, one, one
-        for block in range(blocks):
-            mirror = blocks - 1 - block
-            value_l[tile, pl.ds(block, 1), :] = left
-            step_l[tile, pl.ds(block, 1), :] = left_step
-            value_r[tile, pl.ds(mirror + 1, 1), :] = right
-            step_r[tile, pl.ds(mirror + 1, 1), :] = right_step
-            c, d, e, f = (move[tile, pl.ds(block, 1), :] for move in moves)
-            kept = e * left + f * left_step
-            left_step = c * left + d * left_step
-            left = kept + left_step
-            c, d, e, f = (move[tile, pl.ds(mirror, 1), :] for move in moves)
-            kept = d * right + f * right_step
-            right_step = c * right + e * right_step
-            right = kept + right_step
-        value_l[tile, pl.ds(blocks, 1), :] = left
-        step_l[tile, pl.ds(blocks, 1), :] = left_step
-        value_r[tile, pl.ds(0, 1), :] = right
-        step_r[tile, pl.ds(0, 1), :] = right_step
+        row = pl.ds(blocks, 1)
+        value_l[tile, row, :], step_l[tile, row, :] = lefts[tile]
+        row = pl.ds(0, 1)
+        value_r[tile, row, :], step_r[tile, row, :] = rights[tile]
+        state = value_l[tile, even, :], step_l[tile, even, :]
+        state = onward(state, tuple(move[tile, even, :] for move in moves))
+        value_l[tile, odd, :], step_l[tile, odd, :] = state
+        state = value_r[tile, after, :], step_r[tile, after, :]
+        c, d, e, f = (move[tile, odd, :] for move in moves)
+        value_r[tile, odd, :], step_r[tile, odd, :] = onward(state, (c, e, d, f))
     for tile in range(tiles):
         near = pl.ds(0, blocks)
         far = pl.ds(1, blocks)
@@ -224,18 +244,27 @@
         at = value_r[tile, far, :]
         ratio_r[tile] = at * inverse
         add_r[tile] = first + (at - step_r[tile, far, :]) * inverse * last
+        before, behind = ratio_l[tile, odd, :], ratio_r[tile, even, :]
+        joined[0][tile] = before * ratio_l[tile, even, :]
+        joined[1][tile] = before * add_l[tile, even, :] + add_l[tile, odd, :]
+        joined[2][tile] = behind * ratio_r[tile, odd, :]
+        joined[3][tile] = behind * add_r[tile, odd, :] + add_r[tile, even, :]
+    lefts = [jnp.zeros_like(one)] * tiles
+    rights = [jnp.zeros_like(one)] * tiles
+    for pair in range(pairs):
+        here, there = pl.ds(pair, 1), pl.ds(pairs - 1 - pair, 1)
+        for tile in range(tiles):
+            sum_l[tile, pl.ds(2 * pair, 1), :] = lefts[tile]
+            sum_r[tile, pl.ds(blocks - 2 * pair, 1), :] = rights[tile]
+            lefts[tile] = joined[0][tile, here, :] * lefts[tile] + joined[1][tile, here, :]
+            rights[tile] = joined[2][tile, there, :] * rights[tile] + joined[3][tile, there, :]
     for tile in range(tiles):
-        left = jnp.zeros_like(one)
-        right = jnp.zeros_like(one)
-        for block in range(blocks):
-            mirror = blocks - 1 - block
-            sum_l[tile, pl.ds(block, 1), :] = left
-            sum_r[tile, pl.ds(mirror + 1, 1), :] = right
-            here, there = pl.ds(block, 1), pl.ds(mirror, 1)
-            left = ratio_l[tile, here, :] * left + add_l[tile, here, :]
-            right = ratio_r[tile, there, :] * right + add_r[tile, there, :]
-        sum_l[tile, pl.ds(blocks, 1), :] = left
-        sum_r[tile, pl.ds(0, 1), :] = right
+        sum_l[tile, pl.ds(blocks, 1), :] = lefts[tile]
+        sum_r[tile, pl.ds(0, 1), :] = rights[tile]
+        sum_l[tile, odd, :] = (
+            ratio_l[tile, even, :] * sum_l[tile, even, :] + add_l[tile, even, :]
+        )
+        sum_r[tile, odd, :] = ratio_r[tile, odd, :] * sum_r[tile, after, :] + add_r[tile, odd, :]
     for tile in range(tiles):
         for side in range(2):
             rows = pl.ds(side, blocks)
@@ -455,17 +484,21 @@
     return lax.all_to_all(blocks, axis, 0, 0, tiled=True).reshape(rows.shape)
 
 
-def solve_lines(send, scale, axis, depth):
+def solve_lines(send, scale, axis, depth, beside=None):
     blocks = lax.axis_size(axis)
+    got = exchange(send, axis)
+    if beside is not None:
+        got, beside = lax.optimization_barrier((got, beside))
     tiles = send.shape[0] // (blocks * ROWS)
     states = pltpu.VMEM((tiles, blocks + CELLS, LANES), jnp.float32)
     terms = pltpu.VMEM((tiles, blocks, LANES), jnp.float32)
+    joins = pltpu.VMEM((tiles, blocks // 2, LANES), jnp.float32)
     ends = call(
         functools.partial(solve_kernel, depth, axis, blocks, tiles),
         struct(2 * blocks * tiles, LANES),
-        [states] * 4 + [terms] * 4 + [states] * 2 + [terms] * 4,
-    )(exchange(send, axis), scale)
-    return exchange(ends, axis)
+        [states] * 4 + [terms] * 4 + [states] * 2 + [terms] * 4 + [joins] * 4,
+    )(got, scale)
+    return exchange(ends, axis), beside
 
 
 def on_device(
@@ -532,7 +565,7 @@
         reactants.T,
         products.T,
     )
-    got_y = solve_lines(send_y, scale, "gy", depth)
+    got_y, packed_x = solve_lines(send_y, scale, "gy", depth, packed_x)
     send_x, sources = call(
         functools.partial(middle_kernel, depth),
         [send, block],
@@ -544,7 +577,7 @@
         ],
         far_in=(3,),
     )(got_y, local_y, ends_y, jacobian, jacobian_near, ends_x, packed_x)
-    got_x = solve_lines(send_x, scale, "gx", depth)
+    got_x, _ = solve_lines(send_x, scale, "gx", depth)
     return call(
         finish_kernel,
         [block],

time: 66.4 us -> 66.1 us (level)
  blocking collectives: 50 us -> 42.6 us
  starting transfers between devices: 3.5 us -> 10.4 us
    all_to_all x3, blocking collectives: 50 us -> 42.6 us  [exchange(): return lax.all_to_all(blocks, axis, 0, 0, tiled=True).reshape(rows.shape)]
    all_to_all x1, starting transfers between devices: 3.5 us -> 10.4 us  [exchange(): return lax.all_to_all(blocks, axis, 0, 0, tiled=True).reshape(rows.shape)]
where the time goes in v8:
time: 66.1 us; the launch traced here: 65.7 us
  blocking collectives  42.6 us (64%)
  starting transfers between devices  10.4 us (16%)
  Pallas kernels  8.59 us (13%)
  waiting for transfers between devices  4.01 us (6%)
    all_to_all x3, blocking collectives, exchange(): return lax.all_to_all(blocks, axis, 0, 0, tiled=True).reshape(rows.shape)  42.6 us
    all_to_all x1, starting transfers between devices, exchange(): return lax.all_to_all(blocks, axis, 0, 0, tiled=True).reshape(rows.shape)  10.4 us
    pallas_call x6, Pallas kernels, run(): pl.pallas_call(kernel, out_shape=out_shape, in_specs=[far if k in far_in...  8.59 us
    all_to_all x1, waiting for transfers between devices, exchange(): return lax.all_to_all(blocks, axis, 0, 0, tiled=True).reshape(rows.shape)  4.01 us
  transfers between devices with their start and end apart: 1, of which 1 were waited for; matrix products, arithmetic and copies ran while one was open for 0% of the time, Pallas kernels for 6%

profile of v8, /device:TPU:8, one launch (start us, length us, event | category | flops | bytes accessed | tf_op | source)
XLA Modules:
  0.0 65.7 jit_solution(261946853905150840)
XLA Ops:
  0.0 1.8 %shard_map.73 = (f32[128,128]{1,0:T(8,128)}, f32[8,128]{1,0:T(8,128)S(1)}) custom-call(f32[8,8,512]{2,1,0:T(8,128)} %cot_from.3, f32[8,8,16]{2,1,0:T(8,128)} %cond_from.3, f32[1,32]{1,0:T(1,128)} %bitcast.21), custom_call_target="tpu_custom_call" | custom-call | tf_op jit(solution)/shard_map/pallas_call | solution.py:30
  1.8 10.4 %all-to-all-start = ((f32[16,8,128]{2,1,0:T(8,128)}), f32[16,8,128]{2,1,0:T(8,128)S(1)}, u32[]{:S(2)}, u32[]{:S(2)}) async-start(f32[16,8,128]{2,1,0:T(8,128)} %bitcast.1), calls=%async_computation | async-start | bytes 131072 | tf_op jit(solution)/shard_map/all_to_all | solution.py:484
  12.2 3.8 %shard_map.74 = (f32[3,1024,128]{2,1,0:T(8,128)}, f32[5,1024,128]{2,1,0:T(8,128)S(1)}, f32[8,8,512]{2,1,0:T(8,128)S(1)}, f32[2,8,8,512]{3,2,1,0:T(8,128)S(1)}, f...) custom-call(f32[8,8,512]{2,1,0:T(8,128)} %cot_from.3, f32[8,8,512]{2,1,0:T(8,128)} %conc_from.1, ...), custom_call_target="tpu_custom_call" | custom-call | tf_op jit(solution)/shard_map/pallas_call | solution.py:30
  16.0 4.0 %all-to-all-done = f32[16,8,128]{2,1,0:T(8,128)S(1)} async-done(((f32[16,8,128]{2,1,0:T(8,128)}), f32[16,8,128]{2,1,0:T(8,128)S(1)}, u32[]{:S(2)}, u32[]{:S(2)}) %all-to-all-start) | async-done | bytes 65568 | tf_op jit(solution)/shard_map/all_to_all | solution.py:484
  20.0 0.3 shard_map.75
  20.3 10.7 %all_to_all.20 = f32[16,4,128]{2,1,0:T(4,128)S(1)} all-to-all(f32[16,4,128]{2,1,0:T(4,128)S(1)} %bitcast.16), channel_id=1, replica_groups=mesh['gx'=32,'gy'=16] {'gy'}, dimensions={0} | all-to-all | bytes 65536 | tf_op jit(solution)/shard_map/all_to_all | solution.py:484
  31.0 1.8 %shard_map.76 = (f32[128,128]{1,0:T(8,128)S(1)}, f32[8,8,512]{2,1,0:T(8,128)S(1)}) custom-call(f32[64,128]{1,0:T(8,128)S(1)} %bitcast.14, f32[8,8,512]{2,1,0:T(8,128)S(1)} %get-tuple-element.22.local_ref, f32[2,8,8,512]{3,2,1,0:T(8,128)S(1)} %get-tuple-element.23.ends_y_ref, f32[3,1024,128]{2,1,0:T(8,128)} %get-tuple-element.24.jacobian_from, ...), custom_call_target="tpu_custom_call" | custom-call | tf_op jit(solution)/shard_map/pallas_call | solution.py:30
  32.8 19.1 %all_to_all.21 = f32[32,4,128]{2,1,0:T(4,128)S(1)} all-to-all(f32[32,4,128]{2,1,0:T(4,128)S(1)} %bitcast.18), channel_id=1, replica_groups=mesh['gx'=32,'gy'=16] {'gx'}, dimensions={0} | all-to-all | bytes 131072 | tf_op jit(solution)/shard_map/all_to_all | solution.py:484
  51.9 0.3 shard_map.77
  52.1 12.9 %all_to_all.22 = f32[32,2,128]{2,1,0:T(2,128)S(1)} all-to-all(f32[32,2,128]{2,1,0:T(2,128)S(1)} %bitcast.15), channel_id=1, replica_groups=mesh['gx'=32,'gy'=16] {'gx'}, dimensions={0} | all-to-all | bytes 65536 | tf_op jit(solution)/shard_map/all_to_all | solution.py:484
  65.0 0.7 %shard_map.78 = f32[8,8,512]{2,1,0:T(8,128)} custom-call(f32[64,128]{1,0:T(8,128)S(1)} %bitcast.17, f32[8,8,512]{2,1,0:T(8,128)S(1)} %get-tuple-element.29.sources_ref, f32[2,8,8,512]{3,2,1,0:T(8,128)S(1)} %get-tuple-element.26.ends_x_ref, f32[8,8,512]{2,1,0:T(8,128)S(1)} %get-tuple-element.30.rates_ref), custom_call_target="tpu_custom_call" | custom-call | tf_op jit(solution)/shard_map/pallas_call | solution.py:30
Async XLA Ops:
  1.8 18.2 %all-to-all-start = ((f32[16,8,128]{2,1,0:T(8,128)}), f32[16,8,128]{2,1,0:T(8,128)S(1)}, u32[]{:S(2)}, u32[]{:S(2)}) async-start(f32[16,8,128]{2,1,0:T(8,128)} %bitcast.1), calls=%async_computation | async-start | bytes 131072 | tf_op jit(solution)/shard_map/all_to_all | solution.py:484

commit v9 on v8

--- a/solution.py
+++ b/solution.py
@@ -144,7 +144,7 @@
         [
             (cond_from, cond_ref),
             (diffusivity_from, diffusivity_ref),
-            *((cot_from.at[pl.ds(k, 2)], cot_ref.at[pl.ds(k, 2)]) for k in range(0, CELLS, 2)),
+            (cot_from, cot_ref),
         ],
         sem,
     )
@@ -462,20 +462,13 @@
     )
 
 
-def finish_kernel(ends_ref, sources_ref, ends_x_ref, rates_ref, out_to, out_ref, sem):
+def finish_kernel(ends_ref, sources_ref, ends_x_ref, rates_ref, out_ref):
     to_first = [ends_x_ref[0, k] for k in range(CELLS)]
     to_last = [ends_x_ref[1, k] for k in range(CELLS)]
     local = local_solution([sources_ref[k] for k in range(CELLS)], to_first, to_last)
     left, right = get_ends(ends_ref)
-    copies = []
     for k in range(CELLS):
         out_ref[k] = (local[k] + to_first[k] * left + to_last[k] * right) * rates_ref[k]
-        if k % 2:
-            pair = pl.ds(k - 1, 2)
-            copies.append(pltpu.make_async_copy(out_ref.at[pair], out_to.at[pair], sem.at[k // 2]))
-            copies[-1].start()
-    for copy in copies:
-        copy.wait()
 
 
 def exchange(rows, axis):
@@ -521,7 +514,7 @@
             pltpu.VMEM(cotangent.shape, jnp.float32),
             pltpu.VMEM(conductance.shape, jnp.float32),
             pltpu.VMEM(diffusivity.shape, jnp.float32),
-            pltpu.SemaphoreType.DMA((6,)),
+            pltpu.SemaphoreType.DMA((3,)),
         ],
         far_in=(0, 1, 2),
     )(cotangent, conductance, diffusivity)
@@ -578,12 +571,7 @@
         far_in=(3,),
     )(got_y, local_y, ends_y, jacobian, jacobian_near, ends_x, packed_x)
     got_x, _ = solve_lines(send_x, scale, "gx", depth)
-    return call(
-        finish_kernel,
-        [block],
-        [pltpu.VMEM(block.shape, jnp.float32), pltpu.SemaphoreType.DMA((CELLS // 2,))],
-        far_out=(0,),
-    )(got_x, sources, ends_x, rates_x)[0]
+    return call(finish_kernel, block)(got_x, sources, ends_x, rates_x)
 
 
 def solution(mesh):

time: 66.1 us -> 66 us (level)
  no operation moved by 1% of the time
where the time goes in v9:
time: 66 us; the launch traced here: 65.7 us
  blocking collectives  42.6 us (65%)
  starting transfers between devices  10.4 us (16%)
  Pallas kernels  8.56 us (13%)
  waiting for transfers between devices  4.01 us (6%)
    all_to_all x3, blocking collectives, exchange(): return lax.all_to_all(blocks, axis, 0, 0, tiled=True).reshape(rows.shape)  42.6 us
    all_to_all x1, starting transfers between devices, exchange(): return lax.all_to_all(blocks, axis, 0, 0, tiled=True).reshape(rows.shape)  10.4 us
    pallas_call x6, Pallas kernels, run(): pl.pallas_call(kernel, out_shape=out_shape, in_specs=[far if k in far_in...  8.56 us
    all_to_all x1, waiting for transfers between devices, exchange(): return lax.all_to_all(blocks, axis, 0, 0, tiled=True).reshape(rows.shape)  4.01 us
  transfers between devices with their start and end apart: 1, of which 1 were waited for; matrix products, arithmetic and copies ran while one was open for 0% of the time, Pallas kernels for 6%

profile of v9, /device:TPU:8, one launch (start us, length us, event | category | flops | bytes accessed | tf_op | source)
XLA Modules:
  0.0 65.7 jit_solution(2847803638547681538)
XLA Ops:
  0.0 1.7 %shard_map.73 = (f32[128,128]{1,0:T(8,128)}, f32[8,128]{1,0:T(8,128)S(1)}) custom-call(f32[8,8,512]{2,1,0:T(8,128)} %cot_from.3, f32[8,8,16]{2,1,0:T(8,128)} %cond_from.3, f32[1,32]{1,0:T(1,128)} %bitcast.21), custom_call_target="tpu_custom_call" | custom-call | tf_op jit(solution)/shard_map/pallas_call | solution.py:30
  1.7 10.4 %all-to-all-start = ((f32[16,8,128]{2,1,0:T(8,128)}), f32[16,8,128]{2,1,0:T(8,128)S(1)}, u32[]{:S(2)}, u32[]{:S(2)}) async-start(f32[16,8,128]{2,1,0:T(8,128)} %bitcast.1), calls=%async_computation | async-start | bytes 131072 | tf_op jit(solution)/shard_map/all_to_all | solution.py:477
  12.2 3.8 %shard_map.74 = (f32[3,1024,128]{2,1,0:T(8,128)}, f32[5,1024,128]{2,1,0:T(8,128)S(1)}, f32[8,8,512]{2,1,0:T(8,128)S(1)}, f32[2,8,8,512]{3,2,1,0:T(8,128)S(1)}, f...) custom-call(f32[8,8,512]{2,1,0:T(8,128)} %cot_from.3, f32[8,8,512]{2,1,0:T(8,128)} %conc_from.1, ...), custom_call_target="tpu_custom_call" | custom-call | tf_op jit(solution)/shard_map/pallas_call | solution.py:30
  16.0 4.0 %all-to-all-done = f32[16,8,128]{2,1,0:T(8,128)S(1)} async-done(((f32[16,8,128]{2,1,0:T(8,128)}), f32[16,8,128]{2,1,0:T(8,128)S(1)}, u32[]{:S(2)}, u32[]{:S(2)}) %all-to-all-start) | async-done | bytes 65568 | tf_op jit(solution)/shard_map/all_to_all | solution.py:477
  20.0 0.3 shard_map.75
  20.2 10.7 %all_to_all.20 = f32[16,4,128]{2,1,0:T(4,128)S(1)} all-to-all(f32[16,4,128]{2,1,0:T(4,128)S(1)} %bitcast.16), channel_id=1, replica_groups=mesh['gx'=32,'gy'=16] {'gy'}, dimensions={0} | all-to-all | bytes 65536 | tf_op jit(solution)/shard_map/all_to_all | solution.py:477
  30.9 1.8 %shard_map.76 = (f32[128,128]{1,0:T(8,128)S(1)}, f32[8,8,512]{2,1,0:T(8,128)S(1)}) custom-call(f32[64,128]{1,0:T(8,128)S(1)} %bitcast.14, f32[8,8,512]{2,1,0:T(8,128)S(1)} %get-tuple-element.22.local_ref, f32[2,8,8,512]{3,2,1,0:T(8,128)S(1)} %get-tuple-element.23.ends_y_ref, f32[3,1024,128]{2,1,0:T(8,128)} %get-tuple-element.24.jacobian_from, ...), custom_call_target="tpu_custom_call" | custom-call | tf_op jit(solution)/shard_map/pallas_call | solution.py:30
  32.7 19.1 %all_to_all.21 = f32[32,4,128]{2,1,0:T(4,128)S(1)} all-to-all(f32[32,4,128]{2,1,0:T(4,128)S(1)} %bitcast.18), channel_id=1, replica_groups=mesh['gx'=32,'gy'=16] {'gx'}, dimensions={0} | all-to-all | bytes 131072 | tf_op jit(solution)/shard_map/all_to_all | solution.py:477
  51.8 0.3 shard_map.77
  52.1 12.9 %all_to_all.22 = f32[32,2,128]{2,1,0:T(2,128)S(1)} all-to-all(f32[32,2,128]{2,1,0:T(2,128)S(1)} %bitcast.15), channel_id=1, replica_groups=mesh['gx'=32,'gy'=16] {'gx'}, dimensions={0} | all-to-all | bytes 65536 | tf_op jit(solution)/shard_map/all_to_all | solution.py:477
  65.0 0.7 %shard_map.78 = f32[8,8,512]{2,1,0:T(8,128)} custom-call(f32[64,128]{1,0:T(8,128)S(1)} %bitcast.17, f32[8,8,512]{2,1,0:T(8,128)S(1)} %get-tuple-element.29.sources_ref, f32[2,8,8,512]{3,2,1,0:T(8,128)S(1)} %get-tuple-element.26.ends_x_ref, f32[8,8,512]{2,1,0:T(8,128)S(1)} %get-tuple-element.30.rates_ref), custom_call_target="tpu_custom_call" | custom-call | tf_op jit(solution)/shard_map/pallas_call | solution.py:30
Async XLA Ops:
  1.7 18.2 %all-to-all-start = ((f32[16,8,128]{2,1,0:T(8,128)}), f32[16,8,128]{2,1,0:T(8,128)S(1)}, u32[]{:S(2)}, u32[]{:S(2)}) async-start(f32[16,8,128]{2,1,0:T(8,128)} %bitcast.1), calls=%async_computation | async-start | bytes 131072 | tf_op jit(solution)/shard_map/all_to_all | solution.py:477
